TPU v7x, 32 devices: a whole 2x2x4 slice. The times are simulated.
32 devices in a mesh: dp: 8 (over y, x, core), seq: 4 (over z).
Axes of the slice: x: 2, y: 2, z: 4, core: 2. Of those that a mesh axis runs over, the one named last changes fastest.
Arguments:
- tokens: bfloat16 [8, 1024, 1024], P('dp', 'seq')
- cotangent: bfloat16 [8, 1024, 1024], P('dp', 'seq'), may hold values from -6 to 6
- valid_length: int32 [8], P('dp'), may hold values from 512 to 1024
- segment_ids: int32 [8, 1024], P('dp'), may hold values from 0 to 3, never falling along the last dimension, each value on 1 to 512 neighbouring positions
- piece_starts: int32 [8, 2], P('dp'), may hold values from 0 to 768, as said below
- norm1_gain: bfloat16 [1024], P(('dp', 'seq')), may hold values from 0.5 to 1.5
- norm1_bias: bfloat16 [1024], P(('dp', 'seq')), may hold values from -3 to 3
- qkv_weight: bfloat16 [1024, 3072], P(('dp', 'seq')), may hold values from -0.1875 to 0.1875
- qv_bias: bfloat16 [2048], P(('dp', 'seq')), may hold values from -3 to 3
- out_weight: bfloat16 [1024, 1024], P(('dp', 'seq')), may hold values from -1.5 to 1.5
- out_bias: bfloat16 [1024], P(('dp', 'seq')), may hold values from -3 to 3
- norm2_gain: bfloat16 [1024], P(('dp', 'seq')), may hold values from 0.5 to 1.5
- norm2_bias: bfloat16 [1024], P(('dp', 'seq')), may hold values from -3 to 3
- up_weight: bfloat16 [1024, 4096], P(('dp', 'seq')), may hold values from -0.1875 to 0.1875
- up_bias: bfloat16 [4096], P(('dp', 'seq')), may hold values from -3 to 3
- down_weight: bfloat16 [4096, 1024], P(('dp', 'seq')), may hold values from -0.09375 to 0.09375
- down_bias: bfloat16 [1024], P(('dp', 'seq')), may hold values from -3 to 3
Outputs:
- output: bfloat16 [8, 1024, 1024], P('dp', 'seq')
- tokens_grad: bfloat16 [8, 1024, 1024], P('dp', 'seq')
- grad_norm1_gain: float32 [1024], P(('dp', 'seq'))
- grad_norm1_bias: float32 [1024], P(('dp', 'seq'))
- grad_qkv_weight: float32 [1024, 3072], P(('dp', 'seq'))
- grad_qv_bias: float32 [2048], P(('dp', 'seq'))
- grad_out_weight: float32 [1024, 1024], P(('dp', 'seq'))
- grad_out_bias: float32 [1024], P(('dp', 'seq'))
- grad_norm2_gain: float32 [1024], P(('dp', 'seq'))
- grad_norm2_bias: float32 [1024], P(('dp', 'seq'))
- grad_up_weight: float32 [1024, 4096], P(('dp', 'seq'))
- grad_up_bias: float32 [4096], P(('dp', 'seq'))
- grad_down_weight: float32 [4096, 1024], P(('dp', 'seq'))
- grad_down_bias: float32 [1024], P(('dp', 'seq'))
- residual_rms: float32 [5], replicated
Inputs may be any that keep to these rules, and one draw needn't show every extreme that they name: `piece_starts`: piece p of a sequence starts at p * 512 plus an offset of 0 to 256, so pieces lie in order and never intersect.
All inputs are finite; a program needn't handle non-finite values.
Results may differ from a plain program's by a relative error of at most 0.012.
Values may be sent and summed in bfloat16 or wider, within the bound.
No kernel may reach another device: no remote copies, remote signals or barrier semaphores. Data moves between devices by JAX's collectives and lax.ppermute only.
A program may use at most 192 MiB of HBM per device.

v0:
```python
import functools

import jax
import jax.numpy as jnp
from jax import lax
from jax.experimental import pallas as pl
from jax.experimental.pallas import tpu as pltpu
from jax.sharding import PartitionSpec as P

HEAD_DIM = 64
PIECE = 256


gelu_scale = 0.7978845608028654
gelu_cubic = 0.044715


def layer_norm_parts(rows_in, gain, shift):
    mean_row = jnp.mean(rows_in, axis=-1, keepdims=True)
    centered = rows_in - mean_row
    inverse = lax.rsqrt(jnp.mean(centered * centered, axis=-1, keepdims=True) + 1e-05)
    unit_rows = centered * inverse
    return (unit_rows * gain + shift, unit_rows, inverse)


def layer_norm_back(grad_in, unit_rows, inverse, gain):
    scaled = grad_in * gain
    back_rows = inverse * (
        scaled
        - jnp.mean(scaled, axis=-1, keepdims=True)
        - unit_rows * jnp.mean(scaled * unit_rows, axis=-1, keepdims=True)
    )
    return (back_rows, jnp.sum(grad_in * unit_rows, axis=0), jnp.sum(grad_in, axis=0))


def gelu_parts(values):
    tangent = jnp.tanh(gelu_scale * (values + gelu_cubic * values * values * values))
    slope = 0.5 * (1.0 + tangent) + 0.5 * values * (1.0 - tangent * tangent) * gelu_scale * (
        1.0 + 3.0 * gelu_cubic * values * values
    )
    return (0.5 * values * (1.0 + tangent), slope)


def piece_labels(positions, starts):
    inside = (positions[:, :, None] >= starts[:, None, :]) & (
        positions[:, :, None] < starts[:, None, :] + PIECE
    )
    labels = jnp.arange(1, starts.shape[1] + 1, dtype=jnp.int32)
    return jnp.sum(jnp.where(inside, labels[None, None, :], 0), axis=2)


def swap(value, axis, bit, size):
    return lax.ppermute(value, axis, [(i, i ^ bit) for i in range(size)])


def doubled(bits):
    order = [0]
    for bit in bits:
        order = order + [at ^ bit for at in order]
    return order


def far_bits(dp_size):
    bits = [1 << i for i in range(1, dp_size.bit_length() - 1)]
    half = (len(bits) + 1) // 2
    return bits, bits[half:] + bits[:half]


def add(left, right):
    return (left.astype(jnp.float32) + right.astype(jnp.float32)).astype(left.dtype)


def by_place(blocks, me):
    out, bit = list(blocks), 1
    while bit < len(out):
        odd = jnp.bitwise_and(me, bit) > 0
        out = [jnp.where(odd, out[i ^ bit], out[i]) for i in range(len(out))]
        bit *= 2
    return out


def pick_columns_body(table, flip_ref, in_ref, out_ref):
    width = out_ref.shape[1] // len(table)
    for i, entry in enumerate(table):
        at = pl.multiple_of(jnp.bitwise_xor(flip_ref[0], entry) * width, width)
        out_ref[:, i * width : (i + 1) * width] = in_ref[:, pl.ds(at, width)]


def pick_columns(rows, table, flip):
    width = rows.shape[1] // len(table)
    if width % 128:
        parts = [
            lax.dynamic_slice_in_dim(rows, jnp.bitwise_xor(flip, entry) * width, width, 1)
            for entry in table
        ]
        return jnp.concatenate(parts, axis=1)
    return pl.pallas_call(
        functools.partial(pick_columns_body, table),
        out_shape=jax.ShapeDtypeStruct(rows.shape, rows.dtype),
        in_specs=[
            pl.BlockSpec(memory_space=pltpu.SMEM),
            pl.BlockSpec(memory_space=pltpu.VMEM),
        ],
        out_specs=pl.BlockSpec(memory_space=pltpu.VMEM),
        name="pick_columns",
    )(flip.reshape(1), rows)


def pick_rows(table, index):
    chosen = index[:, None] == jnp.arange(table.shape[0], dtype=jnp.int32)[None, :]
    return jnp.sum(jnp.where(chosen[:, :, None], table[None], 0.0), axis=1)


def held(value, beside):
    out = lax.optimization_barrier((value,) + tuple(beside))
    return out[0], out[1:]


def place_rows_body(plan, *refs):
    ins, out, held_ref, sems = refs[:-3], refs[-3], refs[-2], refs[-1]
    copies_in, copies_out = [], []
    for i, (source, low, rows, high) in enumerate(plan):
        middle = held_ref.at[high : high + rows, :]
        copies_in.append(
            pltpu.make_async_copy(ins[source].at[low : low + rows, :], middle, sems.at[0, i])
        )
        copies_out.append(
            pltpu.make_async_copy(middle, out.at[high : high + rows, :], sems.at[1, i])
        )
    for copy in copies_in:
        copy.start()
    for copy_in, copy_out in zip(copies_in, copies_out):
        copy_in.wait()
        copy_out.start()
    for copy in copies_out:
        copy.wait()


def place_rows(parts, plan):
    rows, cols = sum(entry[2] for entry in plan), parts[0].shape[1]
    size = rows * cols * parts[0].dtype.itemsize
    return pl.pallas_call(
        functools.partial(place_rows_body, plan),
        out_shape=jax.ShapeDtypeStruct((rows, cols), parts[0].dtype),
        in_specs=[pl.BlockSpec(memory_space=pl.ANY)] * len(parts),
        out_specs=pl.BlockSpec(memory_space=pl.ANY),
        scratch_shapes=[
            pltpu.VMEM((rows, cols), parts[0].dtype),
            pltpu.SemaphoreType.DMA((2, len(plan))),
        ],
        cost_estimate=pl.CostEstimate(flops=0, transcendentals=0, bytes_accessed=2 * size),
        name="place_rows",
    )(*parts)


def spread(piece, dp_size, split):
    rows = piece.shape[0]
    bits_x, bits_y = far_bits(dp_size)
    order = doubled(bits_x)
    parts, plans = (piece,), (bits_x,)
    if split:
        parts, plans = (piece[: rows // 2], piece[rows // 2 :]), (bits_x, bits_y)
    for step in range(len(bits_x)):
        parts = yield tuple(parts)
        got = [swap(part, "dp", bits[step], dp_size) for part, bits in zip(parts, plans)]
        if step + 1 < len(bits_x):
            parts = [jnp.concatenate(pair, axis=0) for pair in zip(parts, got)]
    got = yield tuple(got)
    if split:
        half, order_y, plan = rows // 2, doubled(bits_y), []
        count = len(order) // 2
        for i, at in enumerate(order):
            for side, places in enumerate((order, order_y)):
                j = places.index(at)
                source = side if j < count else 2 + side
                plan.append((source, (j % count) * half, half, (2 * i + side) * half))
        own = place_rows(list(parts) + list(got), plan)
    else:
        own = jnp.concatenate([parts[0], got[0]], axis=0)
    (own,) = yield (own,)
    yield own, swap(own, "dp", 1, dp_size)


def run(stages, values, count):
    for _ in range(count):
        values = stages.send(values)
    return values


def collect(own, odd, dp_size, split):
    bits_x, bits_y = far_bits(dp_size)
    order, count = doubled(bits_x), dp_size // 2
    odd = yield tuple(odd)
    got = [swap(part, "dp", 1, dp_size) for part in odd]
    stacks = [
        (a.reshape(count, -1, a.shape[1]), b.reshape(count, -1, a.shape[1]))
        for a, b in zip(own, got)
    ]
    rows = stacks[0][0].shape[1]

    def taken(which, low, high):
        cols = [
            jnp.concatenate([add(a[i, low:high], b[i, low:high]) for a, b in stacks], axis=1)
            for i in which
        ]
        return jnp.stack(cols)

    plans = [(bits_x, 0, rows)]
    if split:
        plans = [(bits_x, 0, rows // 2), (bits_y, rows // 2, rows)]
    keeps, sends = [], []
    half = count // 2
    for bits, low, high in plans:
        places = [order.index(at) for at in doubled(bits)]
        keeps.append(taken(places[:half], low, high))
        sends.append(taken(places[half:], low, high))
    for step in reversed(range(len(bits_x))):
        sends = yield tuple(sends)
        got = [swap(send, "dp", bits[step], dp_size) for send, (bits, _, _) in zip(sends, plans)]
        if step:
            cut = (1 << step) // 2
            sends = [add(keep[cut:], new[cut:]) for keep, new in zip(keeps, got)]
            keeps = [add(keep[:cut], new[:cut]) for keep, new in zip(keeps, got)]
        else:
            keeps = [add(keep, new)[0] for keep, new in zip(keeps, got)]
    yield (jnp.concatenate(keeps, axis=0),)


def seq_gather(shard, seq_size, earlier=None):
    out, earlier = [shard], list(earlier) if earlier else None
    for k in range(1, seq_size):
        sent = shard
        if earlier:
            sent, (earlier[k],) = held(shard, (earlier[k],))
        out.append(swap(sent, "seq", k, seq_size))
    return out, earlier


def seq_cuts(piece, seq_size, seq_at):
    rows = piece.shape[0] // seq_size
    return tuple(
        lax.dynamic_slice_in_dim(piece, jnp.bitwise_xor(seq_at, k) * rows, rows, 0)
        for k in range(seq_size)
    )


def seq_sum(cuts, seq_size):
    total = cuts[0].astype(jnp.float32)
    for k in range(1, seq_size):
        total = total + swap(cuts[k], "seq", k, seq_size).astype(jnp.float32)
    return total


def dot(left, right):
    return jnp.dot(left, right, preferred_element_type=jnp.float32)


def dot_back(grad, weight):
    return jnp.einsum("rn,kn->rk", grad, weight, preferred_element_type=jnp.float32)


def dot_rows(rows, grad):
    return jnp.einsum("rk,rn->kn", rows, grad, preferred_element_type=jnp.float32)


def apply(rows, pair):
    half = rows.shape[1] // 2
    return dot(rows[:, :half], pair[0]) + dot(rows[:, half:], pair[1])


def apply_back(grad, pair, dtype=jnp.float32):
    return jnp.concatenate([dot_back(grad, part).astype(dtype) for part in pair], axis=1)


def weight_grads(rows, grad):
    half = rows.shape[1] // 2
    return [dot_rows(part, grad).astype(jnp.bfloat16) for part in (rows[:, :half], rows[:, half:])]


def seen(valid_ref, query_ref, key_ref):
    valid = valid_ref[0]
    query_at, query_seg, query_piece = (query_ref[:, i : i + 1] for i in range(3))
    key_at, key_seg, key_piece = (key_ref[i : i + 1, :] for i in range(3))
    together = (query_piece == key_piece) & (query_piece > 0)
    rule_ok = (query_seg == key_seg) & ((key_at <= query_at) | together)
    allowed = (key_at < valid) & ((query_at >= valid) | rule_ok)
    return jnp.where(allowed, 0.0, -1e30)


def one_head(rows, head):
    lane = lax.broadcasted_iota(jnp.int32, rows.shape, 1)
    return jnp.where(lane // HEAD_DIM == head, rows, jnp.zeros_like(rows))


def contract(left, right, dims):
    return lax.dot_general(left, right, (dims, ((), ())), preferred_element_type=jnp.float32)


def attend_body(valid_ref, query_ref, key_ref, q_ref, k_ref, v_ref, out_ref, lse_ref):
    hidden_keys = seen(valid_ref, query_ref, key_ref)
    columns = []
    for at in range(0, q_ref.shape[1], 128):
        pair = slice(at, at + 128)
        query, key, value = q_ref[:, pair], k_ref[:, pair], v_ref[:, pair]
        outs = []
        for head in range(128 // HEAD_DIM):
            raw = contract(one_head(query, head), key, ((1,), (1,)))
            raw = raw * HEAD_DIM ** (-0.5) + hidden_keys
            top = jnp.max(raw, axis=-1, keepdims=True)
            expo = jnp.exp(raw - top)
            total = jnp.sum(expo, axis=-1, keepdims=True)
            probs = (expo * (1.0 / total)).astype(jnp.bfloat16)
            outs.append(contract(probs, value, ((1,), (0,))))
            columns.append(top + jnp.log(total))
        lane = lax.broadcasted_iota(jnp.int32, outs[0].shape, 1)
        out_ref[:, pair] = jnp.where(lane < HEAD_DIM, outs[0], outs[1]).astype(out_ref.dtype)
    for i, column in enumerate(columns):
        lse_ref[:, i : i + 1] = column


def attend_back_body(
    valid_ref, query_ref, key_ref, lse_ref, q_ref, k_ref, v_ref, grad_ref, out_ref, sum_ref
):
    step, group = pl.program_id(0), q_ref.shape[1]
    rows = q_ref.shape[0]

    @pl.when(step == 0)
    def _():
        sum_ref[...] = jnp.zeros_like(sum_ref)

    hidden_keys = seen(valid_ref, query_ref, key_ref)
    at_rows = pl.ds(pl.multiple_of(step * rows, rows), rows)
    scale = HEAD_DIM ** (-0.5)
    for at in range(0, group, 128):
        pair = slice(at, at + 128)
        query, key, value, grad = q_ref[:, pair], k_ref[:, pair], v_ref[:, pair], grad_ref[:, pair]
        grad_query = grad_key = grad_value = 0.0
        for head in range(128 // HEAD_DIM):
            column = at // HEAD_DIM + head
            own_query, own_grad = one_head(query, head), one_head(grad, head)
            raw = contract(own_query, key, ((1,), (1,))) * scale + hidden_keys
            probs = jnp.exp(raw - lse_ref[:, column : column + 1])
            grad_probs = contract(own_grad, value, ((1,), (1,)))
            inner = jnp.sum(probs * grad_probs, axis=-1, keepdims=True)
            grad_scores = (probs * (grad_probs - inner)).astype(jnp.bfloat16)
            grad_value += contract(probs.astype(jnp.bfloat16), own_grad, ((0,), (0,)))
            grad_key += contract(grad_scores, own_query, ((0,), (0,)))
            grad_query += contract(grad_scores, one_head(key, head), ((1,), (0,)))
        out_ref[at_rows, pair] = (grad_query * scale).astype(out_ref.dtype)
        sum_ref[:, pair] += grad_key
        sum_ref[:, group + at : group + at + 128] += grad_value

    @pl.when(step == pl.num_programs(0) - 1)
    def _():
        out_ref[:, group : 2 * group] = (sum_ref[:, :group] * scale).astype(out_ref.dtype)
        out_ref[:, 2 * group :] = sum_ref[:, group:].astype(out_ref.dtype)


def attention_specs(length, group, block):
    whole = lambda column: pl.BlockSpec((length, group), lambda i: (0, column))
    return [
        pl.BlockSpec(memory_space=pltpu.SMEM),
        pl.BlockSpec((block, 3), lambda i: (i, 0)),
        pl.BlockSpec((3, length), lambda i: (0, 0)),
    ], [pl.BlockSpec((block, group), lambda i: (i, 0)), whole(1), whole(2)]


def attend(valid, query_info, key_info, qkv_rows, block=256):
    length, group = qkv_rows.shape[0], qkv_rows.shape[1] // 3
    heads = group // HEAD_DIM
    info_specs, qkv_specs = attention_specs(length, group, block)
    work = heads * length * length
    return pl.pallas_call(
        attend_body,
        grid=(length // block,),
        in_specs=info_specs + qkv_specs,
        out_specs=[
            pl.BlockSpec((block, group), lambda i: (i, 0)),
            pl.BlockSpec((block, heads), lambda i: (i, 0)),
        ],
        out_shape=[
            jax.ShapeDtypeStruct((length, group), jnp.bfloat16),
            jax.ShapeDtypeStruct((length, heads), jnp.float32),
        ],
        cost_estimate=pl.CostEstimate(
            flops=16 * work * HEAD_DIM, transcendentals=work, bytes_accessed=32 * length * group
        ),
        name="attend",
    )(valid, query_info, key_info, qkv_rows, qkv_rows, qkv_rows)


def attend_back(valid, query_info, key_info, lse, qkv_rows, grad_rows, block=256):
    length, group = grad_rows.shape
    heads = group // HEAD_DIM
    info_specs, qkv_specs = attention_specs(length, group, block)
    work = heads * length * length
    return pl.pallas_call(
        attend_back_body,
        grid=(length // block,),
        in_specs=info_specs
        + [pl.BlockSpec((block, heads), lambda i: (i, 0))]
        + qkv_specs
        + [pl.BlockSpec((block, group), lambda i: (i, 0))],
        out_specs=pl.BlockSpec((length, 3 * group), lambda i: (0, 0)),
        out_shape=jax.ShapeDtypeStruct((length, 3 * group), jnp.bfloat16),
        scratch_shapes=[pltpu.VMEM((length, 2 * group), jnp.float32)],
        cost_estimate=pl.CostEstimate(
            flops=40 * work * HEAD_DIM, transcendentals=work, bytes_accessed=64 * length * group
        ),
        name="attend_back",
    )(valid, query_info, key_info, lse, qkv_rows, qkv_rows, qkv_rows, grad_rows)


def per_device(
    tokens,
    cotangent,
    valid_length,
    segment_ids,
    piece_starts,
    norm1_gain,
    norm1_bias,
    qkv_weight,
    qv_bias,
    out_weight,
    out_bias,
    norm2_gain,
    norm2_bias,
    up_weight,
    up_bias,
    down_weight,
    down_bias,
):
    f32, bf16 = jnp.float32, jnp.bfloat16
    _, local_len, width = tokens.shape
    dp_size, seq_size = lax.axis_size("dp"), lax.axis_size("seq")
    dp_at, seq_at = lax.axis_index("dp"), lax.axis_index("seq")
    devices = dp_size * seq_size
    group = width // seq_size

    half_order = doubled(far_bits(dp_size)[0])
    full = half_order + [at ^ 1 for at in half_order]
    back = [full.index(at) for at in range(dp_size)]
    place_in_x = lambda block: sum(
        jnp.where(jnp.bitwise_and(block, 1 << i) > 0, back[1 << i], 0)
        for i in range(dp_size.bit_length() - 1)
    )
    to_x, from_x = (full, dp_at), (back, place_in_x(dp_at))
    in_groups = jnp.bitwise_xor(dp_at, seq_at * (dp_size // seq_size))
    groups_to_x, x_to_groups = (full, in_groups), (back, place_in_x(in_groups))
    index_of = lambda rule: jnp.bitwise_xor(jnp.array(rule[0], jnp.int32), rule[1])

    vectors = (norm1_gain, norm1_bias, qv_bias, out_bias, norm2_gain, norm2_bias, up_bias, down_bias)
    widths = [v.shape[0] for v in vectors]
    rows_one = qkv_weight.shape[0]
    slots = len(vectors) + 1
    in_row = -(-slots // rows_one)
    slot = 128 // in_row
    vec_rows = -(-slots // in_row)

    def slotted(parts):
        rows = []
        for at in range(0, len(parts), in_row):
            row = [
                jnp.pad(v, [(0, 0)] * (v.ndim - 1) + [(0, slot - v.shape[-1])])
                for v in parts[at : at + in_row]
            ]
            row = jnp.concatenate(row, axis=-1) if in_row > 1 else row[0]
            rows.append(jnp.pad(row, [(0, 0)] * (row.ndim - 1) + [(0, 128 - row.shape[-1])]))
        rows = jnp.stack(rows, axis=-2)
        return jnp.pad(rows, [(0, 0)] * (rows.ndim - 2) + [(0, rows_one - rows.shape[-2]), (0, 0)])

    def from_slot(table, which):
        row, low = which // in_row, (which % in_row) * slot
        size = widths[which] if which < len(widths) else 6
        return table[..., row, low : low + size]

    vec_block = slotted(vectors)
    qkv_split = qkv_weight.reshape(rows_one, 3, seq_size, group)

    def qkv_part(k):
        mine = lax.dynamic_index_in_dim(qkv_split, jnp.bitwise_xor(seq_at, k), 2, keepdims=False)
        return jnp.concatenate([mine.reshape(rows_one, 3 * group), vec_block], axis=1)

    first = [qkv_part(0)] + [swap(qkv_part(k), "seq", k, seq_size) for k in range(1, seq_size)]
    own_x = pick_columns(tokens[0], *to_x)
    second, _ = seq_gather(jnp.concatenate([out_weight, up_weight], axis=1), seq_size)
    token_blocks = [own_x]
    for k in range(1, seq_size):
        sent, (first[k], second[k]) = held(own_x, (first[k], second[k]))
        token_blocks.append(swap(sent, "seq", k, seq_size))
    far = dp_size.bit_length() - 2
    stacked = lambda blocks: jnp.concatenate(by_place(blocks, seq_at), axis=0)
    one_parts = spread(stacked(first), dp_size, False)
    one_pair = run(one_parts, next(one_parts), far + 2)
    two_parts = spread(stacked(second), dp_size, True)
    two_sends = run(two_parts, next(two_parts), far - 1)
    token_blocks[0], beside = held(token_blocks[0], tuple(token_blocks[1:]) + two_sends)
    token_blocks = token_blocks[:1] + list(beside[: seq_size - 1])
    got = two_parts.send(beside[seq_size - 1 :])
    third, token_blocks = seq_gather(down_weight, seq_size, token_blocks)
    qkv_pair = [part[:, : 3 * group] for part in one_pair]

    vec_x = jnp.concatenate([part[:, 3 * group :] for part in one_pair], axis=0).astype(f32)
    vec_x = vec_x.reshape(dp_size, seq_size, rows_one, 128)[:, :, :vec_rows]
    vec_n = pick_rows(vec_x.reshape(dp_size, -1), index_of(from_x)).reshape(vec_x.shape)

    field = lambda table, which: from_slot(table, which).reshape(-1)
    gain_one, shift_one, gain_two, shift_two = [field(vec_x, i) for i in (0, 1, 4, 5)]
    qv_full, out_shift, up_shift, down_shift = [field(vec_n, i) for i in (2, 3, 6, 7)]

    starts = [jnp.bitwise_xor(seq_at, k) * local_len for k in range(seq_size)]
    step = jnp.arange(local_len, dtype=jnp.int32)
    place = jnp.concatenate([at + step for at in starts])
    segments = jnp.concatenate(
        [lax.dynamic_slice_in_dim(segment_ids, at, local_len, 1) for at in starts], axis=1
    )
    pieces = piece_labels(place[None, :], piece_starts)
    key_info = jnp.concatenate([place[None], segments, pieces], axis=0)
    query_info = key_info.T
    live_rows = (starts[0] + step < valid_length[0]).astype(f32)[:, None]

    all_x = jnp.concatenate(token_blocks, axis=0).astype(f32)
    normed_one, unit_all, _ = layer_norm_parts(all_x, gain_one, shift_one)
    normed_one = normed_one.astype(bf16)
    half_bias = qv_full.reshape(2, seq_size, group)
    half_bias = lax.dynamic_index_in_dim(half_bias, seq_at, 1, keepdims=False)
    qkv_shift = jnp.concatenate([half_bias[0], jnp.zeros((group,), f32), half_bias[1]])
    qkv_rows = (apply(normed_one, qkv_pair) + qkv_shift).astype(bf16)
    attended_rows, lse_all = attend(valid_length, query_info, key_info, qkv_rows)
    attended_rows, beside = held(attended_rows, tuple(third) + tuple(got))
    third, got = beside[:-2], beside[-2:]
    cut_rows = lambda rows, k: rows[k * local_len : (k + 1) * local_len]
    attended = [cut_rows(attended_rows, 0)] + [
        swap(cut_rows(attended_rows, k), "seq", k, seq_size) for k in range(1, seq_size)
    ]
    own, (piece,) = held(two_parts.send(got)[0], (stacked(third),))
    two_pair = two_parts.send((own,))
    out_pair = [part[:, :width] for part in two_pair]
    up_pair = [part[:, width:] for part in two_pair]
    down_parts = spread(piece, dp_size, True)
    down_sends = run(down_parts, next(down_parts), far - 1)

    attended, down_sends = held(jnp.concatenate(attended, axis=1), down_sends)
    got = down_parts.send(down_sends)
    attended = pick_columns(attended, *groups_to_x)
    branch = apply(attended, out_pair) + out_shift
    tokens_f = tokens[0].astype(f32)
    middle = tokens_f + branch
    middle_x = pick_columns(middle, *to_x)
    normed_two, unit_two, inverse_two = layer_norm_parts(middle_x, gain_two, shift_two)
    normed_two = normed_two.astype(bf16)
    hidden = pick_columns(apply(normed_two, up_pair) + up_shift, *to_x)
    hidden, got = held(hidden, got)
    down_pair = run(down_parts, got, 2)
    gated = gelu_parts(hidden)[0].astype(bf16)
    mlp_out = apply(gated, down_pair) + down_shift
    result = middle + mlp_out
    output = result.astype(bf16)[None]
    squares = [
        jnp.sum(live_rows * entry * entry)
        for entry in (tokens_f, branch, middle, mlp_out, result)
    ]
    slots_at = jnp.arange(6, dtype=jnp.int32)
    counted = sum(
        jnp.where(slots_at == i, value, 0.0)
        for i, value in enumerate(squares + [jnp.sum(live_rows)])
    )

    grad_out = cotangent[0] * live_rows.astype(bf16)
    down_grads = weight_grads(gated, grad_out)
    down_sum = collect([down_grads[0]], [down_grads[1]], dp_size, True)
    grad_out_later, sends = held(grad_out, next(down_sum))
    down_sends = down_sum.send(sends)
    hidden_later, down_sends = held(hidden, down_sends)
    down_sends = down_sum.send(down_sends)
    grad_hidden = apply_back(grad_out_later, down_pair) * gelu_parts(hidden_later)[1]
    grad_hidden = pick_columns(grad_hidden.astype(bf16), *from_x)
    up_grads = weight_grads(normed_two, grad_hidden)
    up_sum = collect([up_grads[0]], [up_grads[1]], dp_size, True)
    grad_hidden_later, sends = held(grad_hidden, next(up_sum))
    up_sends = up_sum.send(sends)
    grad_normed_two, down_sends = held(apply_back(grad_hidden_later, up_pair), down_sends)
    down_sends = down_sum.send(down_sends)
    grad_mid_norm, grad_norm2_gain, grad_norm2_bias = layer_norm_back(
        grad_normed_two, unit_two, inverse_two, gain_two
    )
    grad_mid_norm, up_sends = held(pick_columns(grad_mid_norm, *from_x), up_sends)
    up_sends = up_sum.send(up_sends)
    grad_middle = grad_out.astype(f32) + grad_mid_norm
    grad_branch = grad_middle.astype(bf16)
    out_grads = weight_grads(attended, grad_branch)
    grad_attended = pick_columns(apply_back(grad_branch, out_pair, bf16), *x_to_groups)
    cut_cols = lambda rows, k: rows[:, k * group : (k + 1) * group]
    grad_heads = jnp.concatenate(
        [cut_cols(grad_attended, 0)]
        + [swap(cut_cols(grad_attended, k), "seq", k, seq_size) for k in range(1, seq_size)],
        axis=0,
    )
    down_cuts = seq_cuts(run(down_sum, down_sends, far - 2)[0], seq_size, seq_at)
    grad_heads, sends = held(grad_heads, tuple(run(up_sum, up_sends, far - 2)) + down_cuts)
    up_sends, down_cuts = sends[:2], sends[2:]
    down_blocks = [down_cuts[0]]
    down_blocks += [swap(down_cuts[k], "seq", k, seq_size) for k in range(1, seq_size)]
    grad_qkv = attend_back(valid_length, query_info, key_info, lse_all, qkv_rows, grad_heads)
    up_cuts = seq_cuts(up_sum.send(up_sends)[0], seq_size, seq_at)
    grad_qkv, sends = held(grad_qkv, up_cuts + tuple(down_blocks))
    up_cuts, down_blocks = sends[:seq_size], sends[seq_size:]
    up_blocks = [up_cuts[0]] + [swap(up_cuts[k], "seq", k, seq_size) for k in range(1, seq_size)]
    part_normed = apply_back(grad_qkv, qkv_pair)
    grad_norm1_gain = jnp.sum(part_normed * unit_all, axis=0)
    grad_norm1_bias = jnp.sum(part_normed, axis=0)
    part_normed = part_normed.astype(bf16)
    column_sums = jnp.sum(grad_qkv.astype(f32), axis=0).reshape(3, 1, group)
    grad_qv_bias = lax.dynamic_update_slice(
        jnp.zeros((2, seq_size, group), f32),
        jnp.concatenate([column_sums[:1], column_sums[2:]], axis=0),
        (0, seq_at, 0),
    )
    grad_out_bias = jnp.sum(grad_branch.astype(f32), axis=0)
    grad_up_bias = jnp.sum(grad_hidden.astype(f32), axis=0)
    grad_down_bias = jnp.sum(grad_out.astype(f32), axis=0)
    by_device = lambda v: v.reshape(dp_size, seq_size, -1)
    plain = [by_device(v) for v in (grad_qv_bias, grad_out_bias, grad_up_bias, grad_down_bias)]
    moved = [by_device(v) for v in (grad_norm1_gain, grad_norm1_bias, grad_norm2_gain, grad_norm2_bias)]
    spare = [jnp.zeros((dp_size, seq_size, 1), f32)] * 2
    plain_x = slotted(spare + plain[:2] + spare + plain[2:])
    plain_x = pick_rows(plain_x.reshape(dp_size, -1), index_of(to_x)).reshape(plain_x.shape)
    spare = spare[:1] * 2
    counts = jnp.broadcast_to(counted, (dp_size, seq_size, 6))
    vec_grads = plain_x + slotted(moved[:2] + spare + moved[2:] + spare + [counts])
    vec_grads = vec_grads.astype(bf16).reshape(2, -1, 128)
    qkv_grads = weight_grads(normed_one, grad_qkv)
    one_sum = collect(
        [qkv_grads[0], vec_grads[0], out_grads[0]],
        [qkv_grads[1], vec_grads[1], out_grads[1]],
        dp_size,
        False,
    )
    odd = next(one_sum)
    part_normed, beside = held(part_normed, (odd[0], odd[2]) + tuple(up_blocks))
    up_blocks = beside[2:]
    sends = run(one_sum, (beside[0], odd[1], beside[1]), far + 1)
    one_cuts = seq_cuts(sends[0], seq_size, seq_at)
    parts = [cut_rows(part_normed, 0)]
    parts += [swap(cut_rows(part_normed, k), "seq", k, seq_size) for k in range(1, seq_size)]
    parts[1], one_cuts = held(parts[1], one_cuts)
    one_blocks = [one_cuts[0]]
    one_blocks += [swap(one_cuts[k], "seq", k, seq_size) for k in range(1, seq_size)]
    grad_normed_one = sum(part.astype(f32) for part in parts)
    unit_one, inverse_one = layer_norm_parts(own_x.astype(f32), gain_one, shift_one)[1:]
    grad_in_norm = layer_norm_back(grad_normed_one, unit_one, inverse_one, gain_one)[0]
    tokens_grad = (grad_middle + pick_columns(grad_in_norm, *from_x)).astype(bf16)[None]
    up_grad = sum(block.astype(f32) for block in up_blocks)
    down_grad = sum(block.astype(f32) for block in down_blocks)
    one_blocks = [block.astype(f32) for block in one_blocks]
    qkv_grad = jnp.stack(
        [part.reshape(rows_one, 3, group) for part in by_place([b[:, : 3 * group] for b in one_blocks], seq_at)],
        axis=2,
    ).reshape(rows_one, 3 * width)
    rest_sum = sum(block[:, 3 * group :] for block in one_blocks)
    vec_sum, out_grad = rest_sum[:, :128], rest_sum[:, 128:]
    n1g, n1b, qvb, ob, n2g, n2b, ub, db, counted = [from_slot(vec_sum, i) for i in range(slots)]
    residual_rms = jnp.sqrt(counted[:5] / (counted[5] * width))

    return (
        output,
        tokens_grad,
        n1g,
        n1b,
        qkv_grad,
        qvb,
        out_grad,
        ob,
        n2g,
        n2b,
        up_grad,
        ub,
        down_grad,
        db,
        residual_rms,
    )


def solution(mesh):
    return jax.shard_map(
        per_device,
        mesh=mesh,
        in_specs=(
            P("dp", "seq", None),
            P("dp", "seq", None),
            P("dp"),
            P("dp", None),
            P("dp", None),
            P(("dp", "seq")),
            P(("dp", "seq")),
            P(("dp", "seq"), None),
            P(("dp", "seq")),
            P(("dp", "seq"), None),
            P(("dp", "seq")),
            P(("dp", "seq")),
            P(("dp", "seq")),
            P(("dp", "seq"), None),
            P(("dp", "seq")),
            P(("dp", "seq"), None),
            P(("dp", "seq")),
        ),
        out_specs=(
            P("dp", "seq", None),
            P("dp", "seq", None),
            P(("dp", "seq")),
            P(("dp", "seq")),
            P(("dp", "seq"), None),
            P(("dp", "seq")),
            P(("dp", "seq"), None),
            P(("dp", "seq")),
            P(("dp", "seq")),
            P(("dp", "seq")),
            P(("dp", "seq"), None),
            P(("dp", "seq")),
            P(("dp", "seq"), None),
            P(("dp", "seq")),
            P(),
        ),
        check_vma=False,
    )
```

profile of v0, /device:TPU:0, one launch (start us, length us, event | category | flops | bytes accessed | tf_op | source)
XLA Modules:
  0.0 446.6 jit_solution(10980626960341026483)
XLA Ops:
  2.5 3.1 collective-permute-start.1
  5.6 2.5 collective-permute-start.7
  25.5 3.0 collective-permute-done
  28.5 3.5 collective-permute-start.3
  32.6 9.0 %collective-permute-done.3 = bf16[32,896]{1,0:T(8,128)(2,1)S(1)} collective-permute-done((bf16[32,896]{1,0:T(8,128)(2,1)S(1)}, bf16[32,896]{1,0:T(8,128)(2,1)S(1)}, u32[]{:S(2)}, u32[]{:S(2)}) %collective-permute-start.3) | collective-permute-done | bytes 57376 | tf_op jit(solution)/shard_map/ppermute | solution.py:53
  43.3 3.2 collective-permute-start.5
  50.3 12.0 %collective-permute-done.9 = bf16[64,5120]{1,0:T(8,128)(2,1)S(1)} collective-permute-done((bf16[64,5120]{1,0:T(8,128)(2,1)S(1)}, bf16[64,5120]{1,0:T(8,128)(2,1)S(1)}, u32[]{:S(2)}, u32[]{:S(2)}) %collective-permute-start.9) | collective-permute-done | bytes 655392 | tf_op jit(solution)/shard_map/ppermute | solution.py:53
  65.7 16.3 %collective-permute-done.5 = bf16[256,1024]{1,0:T(8,128)(2,1)S(1)} collective-permute-done((bf16[256,1024]{1,0:T(8,128)(2,1)}, bf16[256,1024]{1,0:T(8,128)(2,1)S(1)}, u32[]{:S(2)}, u32[]{:S(2)}) %collective-permute-start.5) | collective-permute-done | bytes 524320 | tf_op jit(solution)/shard_map/ppermute | solution.py:53
  82.0 9.3 %collective-permute-start.14 = (bf16[128,1024]{1,0:T(8,128)(2,1)}, bf16[128,1024]{1,0:T(8,128)(2,1)}, u32[]{:S(2)}, u32[]{:S(2)}) collective-permute-start(bf16[128,1024]{1,0:T(8,128)(2,1)} %param.34), channel_id=1, source_target_pairs={{0,1},{1,0},{2,3},{3,2},{4,5},{5,4},{6,7},{7,6},{8,9},{9,8},{10,11... | collective-permute-start | bytes 786440 | tf_op jit(solution)/shard_map/ppermute | solution.py:53
  95.7 2.5 fusion.8
  105.1 3.1 fusion.6
  111.8 16.0 %attend.1 = (bf16[1024,256]{1,0:T(8,128)(2,1)}, f32[1024,4]{1,0:T(8,128)}) custom-call(s32[1]{0:T(128)} %copy.105.valid_ref, s32[1024,3]{1,0:T(8,128)} %copy.68.query_ref, s32[3,1024]{1,0:T(4,128)} %pad_add_fusion.key_ref, bf16[1024,768]{1,0:T(8,128)(2,1)} %add_convert_fusion.q_ref.k_ref.v_ref, bf16[1024,768]{1,0:T(8,128)(2,1)} %add_convert_fusion.q_ref.k_ref.v_ref, ...), custom_call_target="tpu_custom_call" | custom-call | flops 4294967296 | bytes 8388608 | tf_op jit(solution)/shard_map/attend/pallas_call | solution.py:373
  127.9 2.6 collective-permute-done.18.refs_3_
  130.4 4.7 %place_rows.2 = bf16[512,5120]{1,0:T(8,128)(2,1)} custom-call(bf16[128,5120]{1,0:T(8,128)(2,1)} %copy-done.15, bf16[128,5120]{1,0:T(8,128)(2,1)} %pad_maximum_fusion.3.refs_1_, bf16[128,5120]{1,0:T(8,128)(2,1)} %collective-permute-done.17.refs_2_, bf16[128,5120]{1,0:T(8,128)(2,1)} %collective-permute-done.18.refs_3_), custom_call_target="tpu_custom_call" | custom-call | bytes 10485760 | tf_op jit(solution)/shard_map/place_rows/pallas_call | solution.py:142
  141.5 3.6 collective-permute-done.21
  145.1 4.8 %collective-permute-start.19 = (bf16[256,256]{1,0:T(8,128)(2,1)S(1)}, bf16[256,256]{1,0:T(8,128)(2,1)S(1)}, u32[]{:S(2)}, u32[]{:S(2)}) collective-permute-start(bf16[256,256]{1,0:T(8,128)(2,1)S(1)} %get-tuple-element.267), channel_id=1, source_target_pairs={{0,1},{1,0},{2,3},{3,2},{4,5},{5,4},{6,7},{7,6},{8,9},{9,8},{10,11... | collective-permute-start | bytes 393224 | tf_op jit(solution)/shard_map/ppermute | solution.py:53
  151.8 2.7 collective-permute-done.19
  164.0 3.1 convert_add_fusion.1
  173.8 3.6 fusion.26
  177.5 5.5 %fusion.in_ref = f32[256,4096]{1,0:T(8,128)} fusion(f32[256,4096]{1,0:T(8,128)S(1)} %fusion.26, bf16[512,5120]{1,0:T(8,128)(2,1)} %collective-permute-done.24, f32[4096]{0:T(1024)S(1)} %bitcast.192, bf16[256,1024]{1,0:T(8,128)(2,1)S(1)} %add_convert_fusion.30), kind=kOutput, calls=%fused_computation.6 | convolution fusion | flops 1075838976 | bytes 12861440 | tf_op jit(solution)/shard_map/dot_general | solution.py:255
  183.0 4.4 pick_columns.11
  187.4 3.5 fusion.13
  190.9 3.3 convolution_convert_fusion.3
  194.2 3.6 place_rows.3
  204.6 2.6 add_convert_fusion.27
  209.5 3.9 fusion.124
  213.4 3.7 fusion.20.in_ref
  217.1 3.1 pick_columns.12
  220.2 5.1 %convolution_convert_fusion.1 = bf16[512,4096]{1,0:T(8,128)(2,1)} fusion(bf16[256,4096]{1,0:T(8,128)(2,1)} %pick_columns.12, bf16[256,1024]{1,0:T(8,128)(2,1)} %copy-done.16), kind=kOutput, calls=%fused_computation.4 | convolution fusion | flops 1075838976 | bytes 6553600 | tf_op jit(solution)/shard_map/rk,rn->kn/dot_general | solution.py:263
  228.8 3.6 fusion.46
  236.2 3.9 fusion.109
  241.9 3.8 fusion.21
  246.7 3.3 convolution_convert_fusion
  252.1 3.5 add_convert_fusion.22
  264.1 5.2 %collective-permute-done.38 = bf16[1,256,1024]{2,1,0:T(8,128)(2,1)} collective-permute-done((bf16[1,256,1024]{2,1,0:T(8,128)(2,1)}, bf16[1,256,1024]{2,1,0:T(8,128)(2,1)}, u32[]{:S(2)}, u32[]{:S(2)}) %collective-permute-start.38) | collective-permute-done | bytes 524320 | tf_op jit(solution)/shard_map/ppermute | solution.py:53
  270.0 2.7 fusion.68
  299.3 3.4 collective-permute-done.33
  306.8 3.1 add_convert_fusion.14
  316.2 19.5 %attend_back.1 = bf16[1024,768]{1,0:T(8,128)(2,1)} custom-call(s32[1]{0:T(128)} %copy.105.valid_ref, s32[1024,3]{1,0:T(8,128)} %copy.68.query_ref, s32[3,1024]{1,0:T(4,128)} %pad_add_fusion.key_ref, f32[1024,4]{1,0:T(8,128)} %get-tuple-element.140.lse_ref, bf16[1024,768]{1,0:T(8,128)(2,1)} %add_convert_fusion.q_ref.k_ref.v_ref, ...), custom_call_target="tpu_custom_call" | custom-call | flops 10737418240 | bytes 16777216 | tf_op jit(solution)/shard_map/attend_back/pallas_call | solution.py:397
  336.5 2.9 fusion.70
  347.3 2.9 collective-permute-start.45
  354.4 2.9 convolution_convert_fusion.7
  358.4 8.3 %collective-permute-done.45 = bf16[32,4096]{1,0:T(8,128)(2,1)} collective-permute-done((bf16[32,4096]{1,0:T(8,128)(2,1)}, bf16[32,4096]{1,0:T(8,128)(2,1)}, u32[]{:S(2)}, u32[]{:S(2)}) %collective-permute-start.45) | collective-permute-done | bytes 262176 | tf_op jit(solution)/shard_map/ppermute | solution.py:53
  376.6 2.9 collective-permute-start.53
  379.6 15.9 %collective-permute-done.51 = bf16[2,128,1920]{2,1,0:T(8,128)(2,1)S(1)} collective-permute-done((bf16[2,128,1920]{2,1,0:T(8,128)(2,1)S(1)}, bf16[2,128,1920]{2,1,0:T(8,128)(2,1)S(1)}, u32[]{:S(2)}, u32[]{:S(2)}) %collective-permute-start.51) | collective-permute-done | bytes 983072 | tf_op jit(solution)/shard_map/ppermute | solution.py:53
  398.2 9.8 %collective-permute-done.52 = bf16[1,128,1920]{2,1,0:T(8,128)(2,1)S(1)} collective-permute-done((bf16[1,128,1920]{2,1,0:T(8,128)(2,1)S(1)}, bf16[1,128,1920]{2,1,0:T(8,128)(2,1)S(1)}, u32[]{:S(2)}, u32[]{:S(2)}) %collective-permute-start.52) | collective-permute-done | bytes 491552 | tf_op jit(solution)/shard_map/ppermute | solution.py:53
  410.4 13.5 %collective-permute-done.53 = bf16[256,1024]{1,0:T(8,128)(2,1)S(1)} collective-permute-done((bf16[256,1024]{1,0:T(8,128)(2,1)S(1)}, bf16[256,1024]{1,0:T(8,128)(2,1)S(1)}, u32[]{:S(2)}, u32[]{:S(2)}) %collective-permute-start.53) | collective-permute-done | bytes 524320 | tf_op jit(solution)/shard_map/ppermute | solution.py:53
  436.5 4.2 collective-permute-done.56
  (419 shorter events, 180.4 us)
Async XLA Ops:
  2.5 30.1 %collective-permute-start.1 = (bf16[32,5120]{1,0:T(8,128)(2,1)S(1)}, bf16[32,5120]{1,0:T(8,128)(2,1)S(1)}, u32[]{:S(2)}, u32[]{:S(2)}) collective-permute-start(bf16[32,5120]{1,0:T(8,128)(2,1)S(1)} %constant_dynamic-update-slice_fusion), channel_id=1, source_target_pairs={{0,1},{1,0},{2,3},{3,2},{4,5},{5,4},{6,7},{7,6},{8,9},{9,8},{10,11... | collective-permute-start | bytes 983048 | tf_op jit(solution)/shard_map/ppermute | solution.py:53
  5.6 27.0 %collective-permute-start.7 = (bf16[32,5120]{1,0:T(8,128)(2,1)S(1)}, bf16[32,5120]{1,0:T(8,128)(2,1)S(1)}, u32[]{:S(2)}, u32[]{:S(2)}) collective-permute-start(bf16[32,5120]{1,0:T(8,128)(2,1)S(1)} %constant_dynamic-update-slice_fusion), channel_id=1, source_target_pairs={{0,3},{1,2},{2,1},{3,0},{4,7},{5,6},{6,5},{7,4},{8,11},{9,10},{10,... | collective-permute-start | bytes 983048 | tf_op jit(solution)/shard_map/ppermute | solution.py:53
  8.1 33.5 %collective-permute-start.4 = (bf16[32,5120]{1,0:T(8,128)(2,1)S(1)}, bf16[32,5120]{1,0:T(8,128)(2,1)S(1)}, u32[]{:S(2)}, u32[]{:S(2)}) collective-permute-start(bf16[32,5120]{1,0:T(8,128)(2,1)S(1)} %constant_dynamic-update-slice_fusion), channel_id=1, source_target_pairs={{0,2},{1,3},{2,0},{3,1},{4,6},{5,7},{6,4},{7,5},{8,10},{9,11},{10,... | collective-permute-start | bytes 983048 | tf_op jit(solution)/shard_map/ppermute | solution.py:53
  14.0 14.5 %collective-permute-start = (bf16[32,896]{1,0:T(8,128)(2,1)S(1)}, bf16[32,896]{1,0:T(8,128)(2,1)S(1)}, u32[]{:S(2)}, u32[]{:S(2)}) collective-permute-start(bf16[32,896]{1,0:T(8,128)(2,1)S(1)} %get-tuple-element.299), channel_id=1, source_target_pairs={{0,1},{1,0},{2,3},{3,2},{4,5},{5,4},{6,7},{7,6},{8,9},{9,8},{10,11... | collective-permute-start | bytes 172040 | tf_op jit(solution)/shard_map/ppermute | solution.py:53
  15.9 16.7 %collective-permute-start.6 = (bf16[32,896]{1,0:T(8,128)(2,1)S(1)}, bf16[32,896]{1,0:T(8,128)(2,1)S(1)}, u32[]{:S(2)}, u32[]{:S(2)}) collective-permute-start(bf16[32,896]{1,0:T(8,128)(2,1)S(1)} %get-tuple-element.298), channel_id=1, source_target_pairs={{0,3},{1,2},{2,1},{3,0},{4,7},{5,6},{6,5},{7,4},{8,11},{9,10},{10,... | collective-permute-start | bytes 172040 | tf_op jit(solution)/shard_map/ppermute | solution.py:53
  28.5 13.1 %collective-permute-start.3 = (bf16[32,896]{1,0:T(8,128)(2,1)S(1)}, bf16[32,896]{1,0:T(8,128)(2,1)S(1)}, u32[]{:S(2)}, u32[]{:S(2)}) collective-permute-start(bf16[32,896]{1,0:T(8,128)(2,1)S(1)} %get-tuple-element.300), channel_id=1, source_target_pairs={{0,2},{1,3},{2,0},{3,1},{4,6},{5,7},{6,4},{7,5},{8,10},{9,11},{10,... | collective-permute-start | bytes 172040 | tf_op jit(solution)/shard_map/ppermute | solution.py:53
  43.3 22.4 %collective-permute-start.2 = (bf16[256,1024]{1,0:T(8,128)(2,1)}, bf16[256,1024]{1,0:T(8,128)(2,1)S(1)}, u32[]{:S(2)}, u32[]{:S(2)}) collective-permute-start(bf16[256,1024]{1,0:T(8,128)(2,1)} %pick_columns.8), channel_id=1, source_target_pairs={{0,1},{1,0},{2,3},{3,2},{4,5},{5,4},{6,7},{7,6},{8,9},{9,8},{10,11... | collective-permute-start | bytes 1572872 | tf_op jit(solution)/shard_map/ppermute | solution.py:53
  43.3 38.7 %collective-permute-start.5 = (bf16[256,1024]{1,0:T(8,128)(2,1)}, bf16[256,1024]{1,0:T(8,128)(2,1)S(1)}, u32[]{:S(2)}, u32[]{:S(2)}) collective-permute-start(bf16[256,1024]{1,0:T(8,128)(2,1)} %pick_columns.8), channel_id=1, source_target_pairs={{0,2},{1,3},{2,0},{3,1},{4,6},{5,7},{6,4},{7,5},{8,10},{9,11},{10,... | collective-permute-start | bytes 1572872 | tf_op jit(solution)/shard_map/ppermute | solution.py:53
  46.6 35.5 %collective-permute-start.8 = (bf16[256,1024]{1,0:T(8,128)(2,1)}, bf16[256,1024]{1,0:T(8,128)(2,1)S(1)}, u32[]{:S(2)}, u32[]{:S(2)}) collective-permute-start(bf16[256,1024]{1,0:T(8,128)(2,1)} %pick_columns.8), channel_id=1, source_target_pairs={{0,3},{1,2},{2,1},{3,0},{4,7},{5,6},{6,5},{7,4},{8,11},{9,10},{10,... | collective-permute-start | bytes 1572872 | tf_op jit(solution)/shard_map/ppermute | solution.py:53
  47.9 14.4 %collective-permute-start.9 = (bf16[64,5120]{1,0:T(8,128)(2,1)S(1)}, bf16[64,5120]{1,0:T(8,128)(2,1)S(1)}, u32[]{:S(2)}, u32[]{:S(2)}) collective-permute-start(bf16[64,5120]{1,0:T(8,128)(2,1)S(1)} %pad_maximum_fusion.13), channel_id=1, source_target_pairs={{0,8},{4,12},{8,0},{12,4},{16,24},{20,28},{24,16},{28,20},{1,9},{5... | collective-permute-start | bytes 1966088 | tf_op jit(solution)/shard_map/ppermute | solution.py:53
  48.6 15.3 %collective-permute-start.10 = (bf16[64,5120]{1,0:T(8,128)(2,1)S(1)}, bf16[64,5120]{1,0:T(8,128)(2,1)S(1)}, u32[]{:S(2)}, u32[]{:S(2)}) collective-permute-start(bf16[64,5120]{1,0:T(8,128)(2,1)S(1)} %pad_maximum_fusion.14), channel_id=1, source_target_pairs={{0,16},{4,20},{8,24},{12,28},{16,0},{20,4},{24,8},{28,12},{1,17},{... | collective-permute-start | bytes 1966088 | tf_op jit(solution)/shard_map/ppermute | solution.py:53
  62.3 33.0 %collective-permute-start.12 = (bf16[256,896]{1,0:T(8,128)(2,1)S(1)}, bf16[256,896]{1,0:T(8,128)(2,1)S(1)}, u32[]{:S(2)}, u32[]{:S(2)}) collective-permute-start(bf16[256,896]{1,0:T(8,128)(2,1)S(1)} %get-tuple-element.276), channel_id=1, source_target_pairs={{0,16},{4,20},{8,24},{12,28},{16,0},{20,4},{24,8},{28,12},{1,17},{... | collective-permute-start | bytes 1376264 | tf_op jit(solution)/shard_map/ppermute | solution.py:53
  82.0 45.8 %collective-permute-start.14 = (bf16[128,1024]{1,0:T(8,128)(2,1)}, bf16[128,1024]{1,0:T(8,128)(2,1)}, u32[]{:S(2)}, u32[]{:S(2)}) collective-permute-start(bf16[128,1024]{1,0:T(8,128)(2,1)} %param.34), channel_id=1, source_target_pairs={{0,1},{1,0},{2,3},{3,2},{4,5},{5,4},{6,7},{7,6},{8,9},{9,8},{10,11... | collective-permute-start | bytes 786440 | tf_op jit(solution)/shard_map/ppermute | solution.py:53
  91.3 36.5 %collective-permute-start.15 = (bf16[128,1024]{1,0:T(8,128)(2,1)}, bf16[128,1024]{1,0:T(8,128)(2,1)}, u32[]{:S(2)}, u32[]{:S(2)}) collective-permute-start(bf16[128,1024]{1,0:T(8,128)(2,1)} %param.34), channel_id=1, source_target_pairs={{0,2},{1,3},{2,0},{3,1},{4,6},{5,7},{6,4},{7,5},{8,10},{9,11},{10,... | collective-permute-start | bytes 786440 | tf_op jit(solution)/shard_map/ppermute | solution.py:53
  92.2 35.6 %collective-permute-start.16 = (bf16[128,1024]{1,0:T(8,128)(2,1)}, bf16[128,1024]{1,0:T(8,128)(2,1)}, u32[]{:S(2)}, u32[]{:S(2)}) collective-permute-start(bf16[128,1024]{1,0:T(8,128)(2,1)} %param.34), channel_id=1, source_target_pairs={{0,3},{1,2},{2,1},{3,0},{4,7},{5,6},{6,5},{7,4},{8,11},{9,10},{10,... | collective-permute-start | bytes 786440 | tf_op jit(solution)/shard_map/ppermute | solution.py:53
  93.7 34.1 %collective-permute-start.17 = (bf16[128,5120]{1,0:T(8,128)(2,1)S(1)}, bf16[128,5120]{1,0:T(8,128)(2,1)}, u32[]{:S(2)}, u32[]{:S(2)}) collective-permute-start(bf16[128,5120]{1,0:T(8,128)(2,1)S(1)} %pad_maximum_fusion.2.refs_0_), channel_id=1, source_target_pairs={{0,16},{4,20},{8,24},{12,28},{16,0},{20,4},{24,8},{28,12},{1,17},{... | collective-permute-start | bytes 3932168 | tf_op jit(solution)/shard_map/ppermute | solution.py:53
  98.9 31.6 %collective-permute-start.18 = (bf16[128,5120]{1,0:T(8,128)(2,1)}, bf16[128,5120]{1,0:T(8,128)(2,1)}, u32[]{:S(2)}, u32[]{:S(2)}) collective-permute-start(bf16[128,5120]{1,0:T(8,128)(2,1)} %pad_maximum_fusion.3.refs_1_), channel_id=1, source_target_pairs={{0,8},{4,12},{8,0},{12,4},{16,24},{20,28},{24,16},{28,20},{1,9},{5... | collective-permute-start | bytes 3932168 | tf_op jit(solution)/shard_map/ppermute | solution.py:53
  136.6 27.3 %collective-permute-start.24 = (bf16[512,5120]{1,0:T(8,128)(2,1)}, bf16[512,5120]{1,0:T(8,128)(2,1)}, u32[]{:S(2)}, u32[]{:S(2)}) collective-permute-start(bf16[512,5120]{1,0:T(8,128)(2,1)} %place_rows.2), channel_id=1, source_target_pairs={{0,4},{4,0},{8,12},{12,8},{16,20},{20,16},{24,28},{28,24},{1,5},{5... | collective-permute-start | bytes 15728648 | tf_op jit(solution)/shard_map/ppermute | solution.py:53
  139.2 16.1 %collective-permute-start.22 = (bf16[256,1024]{1,0:T(8,128)(2,1)S(1)}, bf16[256,1024]{1,0:T(8,128)(2,1)}, u32[]{:S(2)}, u32[]{:S(2)}) collective-permute-start(bf16[256,1024]{1,0:T(8,128)(2,1)S(1)} %get-tuple-element.251), channel_id=1, source_target_pairs={{0,8},{4,12},{8,0},{12,4},{16,24},{20,28},{24,16},{28,20},{1,9},{5... | collective-permute-start | bytes 1572872 | tf_op jit(solution)/shard_map/ppermute | solution.py:53
  139.8 17.7 %collective-permute-start.23 = (bf16[256,1024]{1,0:T(8,128)(2,1)S(1)}, bf16[256,1024]{1,0:T(8,128)(2,1)}, u32[]{:S(2)}, u32[]{:S(2)}) collective-permute-start(bf16[256,1024]{1,0:T(8,128)(2,1)S(1)} %get-tuple-element.250), channel_id=1, source_target_pairs={{0,16},{4,20},{8,24},{12,28},{16,0},{20,4},{24,8},{28,12},{1,17},{... | collective-permute-start | bytes 1572872 | tf_op jit(solution)/shard_map/ppermute | solution.py:53
  141.3 10.5 %collective-permute-start.20 = (bf16[256,256]{1,0:T(8,128)(2,1)S(1)}, bf16[256,256]{1,0:T(8,128)(2,1)S(1)}, u32[]{:S(2)}, u32[]{:S(2)}) collective-permute-start(bf16[256,256]{1,0:T(8,128)(2,1)S(1)} %get-tuple-element.266), channel_id=1, source_target_pairs={{0,2},{1,3},{2,0},{3,1},{4,6},{5,7},{6,4},{7,5},{8,10},{9,11},{10,... | collective-permute-start | bytes 393224 | tf_op jit(solution)/shard_map/ppermute | solution.py:53
  159.7 27.7 %collective-permute-start.25 = (bf16[512,1024]{1,0:T(8,128)(2,1)}, bf16[512,1024]{1,0:T(8,128)(2,1)}, u32[]{:S(2)}, u32[]{:S(2)}) collective-permute-start(bf16[512,1024]{1,0:T(8,128)(2,1)} %pad_maximum_fusion.5.refs_0_), channel_id=1, source_target_pairs={{0,16},{4,20},{8,24},{12,28},{16,0},{20,4},{24,8},{28,12},{1,17},{... | collective-permute-start | bytes 3145736 | tf_op jit(solution)/shard_map/ppermute | solution.py:53
  160.2 27.2 %collective-permute-start.26 = (bf16[512,1024]{1,0:T(8,128)(2,1)}, bf16[512,1024]{1,0:T(8,128)(2,1)}, u32[]{:S(2)}, u32[]{:S(2)}) collective-permute-start(bf16[512,1024]{1,0:T(8,128)(2,1)} %pad_maximum_fusion.6.refs_1_), channel_id=1, source_target_pairs={{0,8},{4,12},{8,0},{12,4},{16,24},{20,28},{24,16},{28,20},{1,9},{5... | collective-permute-start | bytes 3145736 | tf_op jit(solution)/shard_map/ppermute | solution.py:53
  194.2 10.4 %collective-permute-start.28 = (bf16[2048,1024]{1,0:T(8,128)(2,1)}, bf16[2048,1024]{1,0:T(8,128)(2,1)}, u32[]{:S(2)}, u32[]{:S(2)}) collective-permute-start(bf16[2048,1024]{1,0:T(8,128)(2,1)} %convolution_convert_fusion.3), channel_id=1, source_target_pairs={{0,4},{4,0},{8,12},{12,8},{16,20},{20,16},{24,28},{28,24},{1,5},{5... | collective-permute-start | bytes 12582920 | tf_op jit(solution)/shard_map/ppermute | solution.py:53
  197.8 11.7 %collective-permute-start.27 = (bf16[2048,1024]{1,0:T(8,128)(2,1)}, bf16[2048,1024]{1,0:T(8,128)(2,1)}, u32[]{:S(2)}, u32[]{:S(2)}) collective-permute-start(bf16[2048,1024]{1,0:T(8,128)(2,1)} %place_rows.3), channel_id=1, source_target_pairs={{0,4},{4,0},{8,12},{12,8},{16,20},{20,16},{24,28},{28,24},{1,5},{5... | collective-permute-start | bytes 12582920 | tf_op jit(solution)/shard_map/ppermute | solution.py:53
  225.3 25.4 %collective-permute-start.30 = (bf16[2,256,1024]{2,1,0:T(8,128)(2,1)S(1)}, bf16[2,256,1024]{2,1,0:T(8,128)(2,1)S(1)}, u32[]{:S(2)}, u32[]{:S(2)}) collective-permute-start(bf16[2,256,1024]{2,1,0:T(8,128)(2,1)S(1)} %copy-done.31), channel_id=1, source_target_pairs={{0,8},{4,12},{8,0},{12,4},{16,24},{20,28},{24,16},{28,20},{1,9},{5... | collective-permute-start | bytes 3145736 | tf_op jit(solution)/shard_map/ppermute | solution.py:53
  227.2 24.8 %collective-permute-start.29 = (bf16[2,256,1024]{2,1,0:T(8,128)(2,1)S(1)}, bf16[2,256,1024]{2,1,0:T(8,128)(2,1)S(1)}, u32[]{:S(2)}, u32[]{:S(2)}) collective-permute-start(bf16[2,256,1024]{2,1,0:T(8,128)(2,1)S(1)} %copy-done.30), channel_id=1, source_target_pairs={{0,16},{4,20},{8,24},{12,28},{16,0},{20,4},{24,8},{28,12},{1,17},{... | collective-permute-start | bytes 3145736 | tf_op jit(solution)/shard_map/ppermute | solution.py:53
  228.8 46.3 %collective-permute-start.31 = (bf16[512,4096]{1,0:T(8,128)(2,1)}, bf16[512,4096]{1,0:T(8,128)(2,1)}, u32[]{:S(2)}, u32[]{:S(2)}) collective-permute-start(bf16[512,4096]{1,0:T(8,128)(2,1)} %convolution_convert_fusion.1), channel_id=1, source_target_pairs={{0,4},{4,0},{8,12},{12,8},{16,20},{20,16},{24,28},{28,24},{1,5},{5... | collective-permute-start | bytes 12582920 | tf_op jit(solution)/shard_map/ppermute | solution.py:53
  255.6 13.7 %collective-permute-start.38 = (bf16[1,256,1024]{2,1,0:T(8,128)(2,1)}, bf16[1,256,1024]{2,1,0:T(8,128)(2,1)}, u32[]{:S(2)}, u32[]{:S(2)}) collective-permute-start(bf16[1,256,1024]{2,1,0:T(8,128)(2,1)} %get-tuple-element.144), channel_id=1, source_target_pairs={{0,16},{4,20},{8,24},{12,28},{16,0},{20,4},{24,8},{28,12},{1,17},{... | collective-permute-start | bytes 1572872 | tf_op jit(solution)/shard_map/ppermute | solution.py:53
  257.2 12.8 %collective-permute-start.37 = (bf16[1,256,1024]{2,1,0:T(8,128)(2,1)}, bf16[1,256,1024]{2,1,0:T(8,128)(2,1)}, u32[]{:S(2)}, u32[]{:S(2)}) collective-permute-start(bf16[1,256,1024]{2,1,0:T(8,128)(2,1)} %get-tuple-element.143), channel_id=1, source_target_pairs={{0,8},{4,12},{8,0},{12,4},{16,24},{20,28},{24,16},{28,20},{1,9},{5... | collective-permute-start | bytes 1572872 | tf_op jit(solution)/shard_map/ppermute | solution.py:53
  282.1 23.4 %collective-permute-start.36 = (bf16[2,64,4096]{2,1,0:T(8,128)(2,1)}, bf16[2,64,4096]{2,1,0:T(8,128)(2,1)}, u32[]{:S(2)}, u32[]{:S(2)}) collective-permute-start(bf16[2,64,4096]{2,1,0:T(8,128)(2,1)} %pad_maximum_fusion.11), channel_id=1, source_target_pairs={{0,8},{4,12},{8,0},{12,4},{16,24},{20,28},{24,16},{28,20},{1,9},{5... | collective-permute-start | bytes 3145736 | tf_op jit(solution)/shard_map/ppermute | solution.py:53
  283.7 23.2 %collective-permute-start.35 = (bf16[2,64,4096]{2,1,0:T(8,128)(2,1)}, bf16[2,64,4096]{2,1,0:T(8,128)(2,1)}, u32[]{:S(2)}, u32[]{:S(2)}) collective-permute-start(bf16[2,64,4096]{2,1,0:T(8,128)(2,1)} %pad_maximum_fusion.10), channel_id=1, source_target_pairs={{0,16},{4,20},{8,24},{12,28},{16,0},{20,4},{24,8},{28,12},{1,17},{... | collective-permute-start | bytes 3145736 | tf_op jit(solution)/shard_map/ppermute | solution.py:53
  292.9 9.8 %collective-permute-start.33 = (bf16[256,256]{1,0:T(8,128)(2,1)}, bf16[256,256]{1,0:T(8,128)(2,1)}, u32[]{:S(2)}, u32[]{:S(2)}) collective-permute-start(bf16[256,256]{1,0:T(8,128)(2,1)} %get-tuple-element.262), channel_id=1, source_target_pairs={{0,2},{1,3},{2,0},{3,1},{4,6},{5,7},{6,4},{7,5},{8,10},{9,11},{10,... | collective-permute-start | bytes 393224 | tf_op jit(solution)/shard_map/ppermute | solution.py:53
  310.0 25.7 %collective-permute-start.40 = (bf16[1,64,4096]{2,1,0:T(8,128)(2,1)}, bf16[1,64,4096]{2,1,0:T(8,128)(2,1)S(1)}, u32[]{:S(2)}, u32[]{:S(2)}) collective-permute-start(bf16[1,64,4096]{2,1,0:T(8,128)(2,1)} %get-tuple-element.147), channel_id=1, source_target_pairs={{0,16},{4,20},{8,24},{12,28},{16,0},{20,4},{24,8},{28,12},{1,17},{... | collective-permute-start | bytes 1572872 | tf_op jit(solution)/shard_map/ppermute | solution.py:53
  310.5 26.0 %collective-permute-start.39 = (bf16[1,64,4096]{2,1,0:T(8,128)(2,1)S(1)}, bf16[1,64,4096]{2,1,0:T(8,128)(2,1)}, u32[]{:S(2)}, u32[]{:S(2)}) collective-permute-start(bf16[1,64,4096]{2,1,0:T(8,128)(2,1)S(1)} %get-tuple-element.146), channel_id=1, source_target_pairs={{0,8},{4,12},{8,0},{12,4},{16,24},{20,28},{24,16},{28,20},{1,9},{5... | collective-permute-start | bytes 1572872 | tf_op jit(solution)/shard_map/ppermute | solution.py:53
  311.8 29.0 %collective-permute-start.41 = (bf16[128,1024]{1,0:T(8,128)(2,1)}, bf16[128,1024]{1,0:T(8,128)(2,1)}, u32[]{:S(2)}, u32[]{:S(2)}) collective-permute-start(bf16[128,1024]{1,0:T(8,128)(2,1)} %get-tuple-element.149), channel_id=1, source_target_pairs={{0,1},{1,0},{2,3},{3,2},{4,5},{5,4},{6,7},{7,6},{8,9},{9,8},{10,11... | collective-permute-start | bytes 786440 | tf_op jit(solution)/shard_map/ppermute | solution.py:53
  312.2 28.6 %collective-permute-start.42 = (bf16[128,1024]{1,0:T(8,128)(2,1)}, bf16[128,1024]{1,0:T(8,128)(2,1)}, u32[]{:S(2)}, u32[]{:S(2)}) collective-permute-start(bf16[128,1024]{1,0:T(8,128)(2,1)} %get-tuple-element.150), channel_id=1, source_target_pairs={{0,2},{1,3},{2,0},{3,1},{4,6},{5,7},{6,4},{7,5},{8,10},{9,11},{10,... | collective-permute-start | bytes 786440 | tf_op jit(solution)/shard_map/ppermute | solution.py:53
  314.7 26.2 %collective-permute-start.43 = (bf16[128,1024]{1,0:T(8,128)(2,1)}, bf16[128,1024]{1,0:T(8,128)(2,1)}, u32[]{:S(2)}, u32[]{:S(2)}) collective-permute-start(bf16[128,1024]{1,0:T(8,128)(2,1)} %get-tuple-element.151), channel_id=1, source_target_pairs={{0,3},{1,2},{2,1},{3,0},{4,7},{5,6},{6,5},{7,4},{8,11},{9,10},{10,... | collective-permute-start | bytes 786440 | tf_op jit(solution)/shard_map/ppermute | solution.py:53
  347.3 11.1 %collective-permute-start.44 = (bf16[32,4096]{1,0:T(8,128)(2,1)}, bf16[32,4096]{1,0:T(8,128)(2,1)}, u32[]{:S(2)}, u32[]{:S(2)}) collective-permute-start(bf16[32,4096]{1,0:T(8,128)(2,1)} %get-tuple-element.154), channel_id=1, source_target_pairs={{0,1},{1,0},{2,3},{3,2},{4,5},{5,4},{6,7},{7,6},{8,9},{9,8},{10,11... | collective-permute-start | bytes 786440 | tf_op jit(solution)/shard_map/ppermute | solution.py:53
  347.3 19.3 %collective-permute-start.45 = (bf16[32,4096]{1,0:T(8,128)(2,1)}, bf16[32,4096]{1,0:T(8,128)(2,1)}, u32[]{:S(2)}, u32[]{:S(2)}) collective-permute-start(bf16[32,4096]{1,0:T(8,128)(2,1)} %get-tuple-element.155), channel_id=1, source_target_pairs={{0,2},{1,3},{2,0},{3,1},{4,6},{5,7},{6,4},{7,5},{8,10},{9,11},{10,... | collective-permute-start | bytes 786440 | tf_op jit(solution)/shard_map/ppermute | solution.py:53
  350.2 16.5 %collective-permute-start.46 = (bf16[32,4096]{1,0:T(8,128)(2,1)}, bf16[32,4096]{1,0:T(8,128)(2,1)}, u32[]{:S(2)}, u32[]{:S(2)}) collective-permute-start(bf16[32,4096]{1,0:T(8,128)(2,1)} %get-tuple-element.156), channel_id=1, source_target_pairs={{0,3},{1,2},{2,1},{3,0},{4,7},{5,6},{6,5},{7,4},{8,11},{9,10},{10,... | collective-permute-start | bytes 786440 | tf_op jit(solution)/shard_map/ppermute | solution.py:53
  371.6 23.9 %collective-permute-start.51 = (bf16[2,128,1920]{2,1,0:T(8,128)(2,1)S(1)}, bf16[2,128,1920]{2,1,0:T(8,128)(2,1)S(1)}, u32[]{:S(2)}, u32[]{:S(2)}) collective-permute-start(bf16[2,128,1920]{2,1,0:T(8,128)(2,1)S(1)} %pad_maximum_fusion.12), channel_id=1, source_target_pairs={{0,16},{4,20},{8,24},{12,28},{16,0},{20,4},{24,8},{28,12},{1,17},{... | collective-permute-start | bytes 2949128 | tf_op jit(solution)/shard_map/ppermute | solution.py:53
  374.6 35.8 %collective-permute-start.54 = (bf16[256,1024]{1,0:T(8,128)(2,1)S(1)}, bf16[256,1024]{1,0:T(8,128)(2,1)S(1)}, u32[]{:S(2)}, u32[]{:S(2)}) collective-permute-start(bf16[256,1024]{1,0:T(8,128)(2,1)S(1)} %get-tuple-element.232), channel_id=1, source_target_pairs={{0,3},{1,2},{2,1},{3,0},{4,7},{5,6},{6,5},{7,4},{8,11},{9,10},{10,... | collective-permute-start | bytes 1572872 | tf_op jit(solution)/shard_map/ppermute | solution.py:53
  376.6 47.2 %collective-permute-start.53 = (bf16[256,1024]{1,0:T(8,128)(2,1)S(1)}, bf16[256,1024]{1,0:T(8,128)(2,1)S(1)}, u32[]{:S(2)}, u32[]{:S(2)}) collective-permute-start(bf16[256,1024]{1,0:T(8,128)(2,1)S(1)} %get-tuple-element.233), channel_id=1, source_target_pairs={{0,2},{1,3},{2,0},{3,1},{4,6},{5,7},{6,4},{7,5},{8,10},{9,11},{10,... | collective-permute-start | bytes 1572872 | tf_op jit(solution)/shard_map/ppermute | solution.py:53
  379.6 30.8 %collective-permute-start.47 = (bf16[256,1024]{1,0:T(8,128)(2,1)S(1)}, bf16[256,1024]{1,0:T(8,128)(2,1)S(1)}, u32[]{:S(2)}, u32[]{:S(2)}) collective-permute-start(bf16[256,1024]{1,0:T(8,128)(2,1)S(1)} %get-tuple-element.231), channel_id=1, source_target_pairs={{0,1},{1,0},{2,3},{3,2},{4,5},{5,4},{6,7},{7,6},{8,9},{9,8},{10,11... | collective-permute-start | bytes 1572872 | tf_op jit(solution)/shard_map/ppermute | solution.py:53
  395.6 12.5 %collective-permute-start.52 = (bf16[1,128,1920]{2,1,0:T(8,128)(2,1)S(1)}, bf16[1,128,1920]{2,1,0:T(8,128)(2,1)S(1)}, u32[]{:S(2)}, u32[]{:S(2)}) collective-permute-start(bf16[1,128,1920]{2,1,0:T(8,128)(2,1)S(1)} %add_convert_fusion.32), channel_id=1, source_target_pairs={{0,8},{4,12},{8,0},{12,4},{16,24},{20,28},{24,16},{28,20},{1,9},{5... | collective-permute-start | bytes 1474568 | tf_op jit(solution)/shard_map/ppermute | solution.py:53
  430.1 10.5 %collective-permute-start.56 = (bf16[32,1920]{1,0:T(8,128)(2,1)S(1)}, bf16[32,1920]{1,0:T(8,128)(2,1)S(1)}, u32[]{:S(2)}, u32[]{:S(2)}) collective-permute-start(bf16[32,1920]{1,0:T(8,128)(2,1)S(1)} %get-tuple-element.163), channel_id=1, source_target_pairs={{0,2},{1,3},{2,0},{3,1},{4,6},{5,7},{6,4},{7,5},{8,10},{9,11},{10,... | collective-permute-start | bytes 368648 | tf_op jit(solution)/shard_map/ppermute | solution.py:53
  430.2 10.6 %collective-permute-start.55 = (bf16[32,1920]{1,0:T(8,128)(2,1)S(1)}, bf16[32,1920]{1,0:T(8,128)(2,1)S(1)}, u32[]{:S(2)}, u32[]{:S(2)}) collective-permute-start(bf16[32,1920]{1,0:T(8,128)(2,1)S(1)} %get-tuple-element.162), channel_id=1, source_target_pairs={{0,1},{1,0},{2,3},{3,2},{4,5},{5,4},{6,7},{7,6},{8,9},{9,8},{10,11... | collective-permute-start | bytes 368648 | tf_op jit(solution)/shard_map/ppermute | solution.py:53
  (74 other events, 662.1 us)
where the time goes:
time: 452 us; the launch traced here: 447 us
  waiting for transfers between devices  122 us (27%)
  other arithmetic  86.8 us (19%)
  starting transfers between devices  81.5 us (18%)
  Pallas kernels  64.5 us (14%)
  matrix products  57.7 us (13%)
  local copies, waits for them, and re-layouts  30.6 us (7%)
    ppermute x58, waiting for transfers between devices, swap(): return lax.ppermute(value, axis, [(i, i ^ bit) for i in range(size)])  122 us
    ppermute x58, starting transfers between devices, swap(): return lax.ppermute(value, axis, [(i, i ^ bit) for i in range(size)])  81.5 us
    dot_general x8, matrix products, dot(): return jnp.dot(left, right, preferred_element_type=jnp.float32)  22 us
    pallas_call x8, Pallas kernels, pick_columns(): pl.pallas_call(functools.partial(pick_columns_body, table), out_shape=jax...  20.7 us
    dot_general x8, matrix products, dot_rows(): jnp.einsum('rk,rn->kn', rows, grad, preferred_element_type=jnp.float32)  19.9 us
    pallas_call x1, Pallas kernels, attend_back(): pl.pallas_call(attend_back_body, grid=(length // block,), in_specs=info_s...  19.5 us
    pallas_call x1, Pallas kernels, attend(): pl.pallas_call(attend_body, grid=(length // block,), in_specs=info_specs...  16 us
    dot_general x8, matrix products, dot_back(): jnp.einsum('rn,kn->rk', grad, weight, preferred_element_type=jnp.float32)  15.7 us
  transfers between devices with their start and end apart: 58, of which 25 were waited for; matrix products, arithmetic and copies ran while one was open for 28% of the time, Pallas kernels for 12%

commit v1 on v0

--- a/solution.py
+++ b/solution.py
@@ -244,13 +244,6 @@
     )
 
 
-def seq_sum(cuts, seq_size):
-    total = cuts[0].astype(jnp.float32)
-    for k in range(1, seq_size):
-        total = total + swap(cuts[k], "seq", k, seq_size).astype(jnp.float32)
-    return total
-
-
 def dot(left, right):
     return jnp.dot(left, right, preferred_element_type=jnp.float32)
 
@@ -466,7 +459,9 @@
             ]
             row = jnp.concatenate(row, axis=-1) if in_row > 1 else row[0]
             rows.append(jnp.pad(row, [(0, 0)] * (row.ndim - 1) + [(0, 128 - row.shape[-1])]))
-        rows = jnp.stack(rows, axis=-2)
+        return jnp.stack(rows, axis=-2)
+
+    def whole_rows(rows):
         return jnp.pad(rows, [(0, 0)] * (rows.ndim - 2) + [(0, rows_one - rows.shape[-2]), (0, 0)])
 
     def from_slot(table, which):
@@ -474,7 +469,7 @@
         size = widths[which] if which < len(widths) else 6
         return table[..., row, low : low + size]
 
-    vec_block = slotted(vectors)
+    vec_block = whole_rows(slotted(vectors))
     qkv_split = qkv_weight.reshape(rows_one, 3, seq_size, group)
 
     def qkv_part(k):
@@ -553,19 +548,6 @@
     hidden, got = held(hidden, got)
     down_pair = run(down_parts, got, 2)
     gated = gelu_parts(hidden)[0].astype(bf16)
-    mlp_out = apply(gated, down_pair) + down_shift
-    result = middle + mlp_out
-    output = result.astype(bf16)[None]
-    squares = [
-        jnp.sum(live_rows * entry * entry)
-        for entry in (tokens_f, branch, middle, mlp_out, result)
-    ]
-    slots_at = jnp.arange(6, dtype=jnp.int32)
-    counted = sum(
-        jnp.where(slots_at == i, value, 0.0)
-        for i, value in enumerate(squares + [jnp.sum(live_rows)])
-    )
-
     grad_out = cotangent[0] * live_rows.astype(bf16)
     down_grads = weight_grads(gated, grad_out)
     down_sum = collect([down_grads[0]], [down_grads[1]], dp_size, True)
@@ -579,33 +561,41 @@
     up_sum = collect([up_grads[0]], [up_grads[1]], dp_size, True)
     grad_hidden_later, sends = held(grad_hidden, next(up_sum))
     up_sends = up_sum.send(sends)
-    grad_normed_two, down_sends = held(apply_back(grad_hidden_later, up_pair), down_sends)
-    down_sends = down_sum.send(down_sends)
+    grad_normed_two = apply_back(grad_hidden_later, up_pair)
     grad_mid_norm, grad_norm2_gain, grad_norm2_bias = layer_norm_back(
         grad_normed_two, unit_two, inverse_two, gain_two
     )
-    grad_mid_norm, up_sends = held(pick_columns(grad_mid_norm, *from_x), up_sends)
-    up_sends = up_sum.send(up_sends)
+    grad_mid_norm = pick_columns(grad_mid_norm, *from_x)
     grad_middle = grad_out.astype(f32) + grad_mid_norm
     grad_branch = grad_middle.astype(bf16)
     out_grads = weight_grads(attended, grad_branch)
     grad_attended = pick_columns(apply_back(grad_branch, out_pair, bf16), *x_to_groups)
+    grad_attended, (gated_later,) = held(grad_attended, (gated,))
+    mlp_out = apply(gated_later, down_pair) + down_shift
+    result = middle + mlp_out
+    output = result.astype(bf16)[None]
+    squares = [
+        jnp.sum(live_rows * entry * entry)
+        for entry in (tokens_f, branch, middle, mlp_out, result)
+    ]
+    slots_at = jnp.arange(6, dtype=jnp.int32)
+    counted = sum(
+        jnp.where(slots_at == i, value, 0.0)
+        for i, value in enumerate(squares + [jnp.sum(live_rows)])
+    )
     cut_cols = lambda rows, k: rows[:, k * group : (k + 1) * group]
     grad_heads = jnp.concatenate(
         [cut_cols(grad_attended, 0)]
         + [swap(cut_cols(grad_attended, k), "seq", k, seq_size) for k in range(1, seq_size)],
         axis=0,
     )
-    down_cuts = seq_cuts(run(down_sum, down_sends, far - 2)[0], seq_size, seq_at)
-    grad_heads, sends = held(grad_heads, tuple(run(up_sum, up_sends, far - 2)) + down_cuts)
-    up_sends, down_cuts = sends[:2], sends[2:]
+    grad_heads, sends = held(grad_heads, tuple(down_sends) + tuple(up_sends))
+    down_cuts = seq_cuts(run(down_sum, sends[:2], far - 1)[0], seq_size, seq_at)
+    up_sends = run(up_sum, sends[2:], far - 1)
+    grad_qkv = attend_back(valid_length, query_info, key_info, lse_all, qkv_rows, grad_heads)
+    grad_qkv, down_cuts = held(grad_qkv, down_cuts)
     down_blocks = [down_cuts[0]]
     down_blocks += [swap(down_cuts[k], "seq", k, seq_size) for k in range(1, seq_size)]
-    grad_qkv = attend_back(valid_length, query_info, key_info, lse_all, qkv_rows, grad_heads)
-    up_cuts = seq_cuts(up_sum.send(up_sends)[0], seq_size, seq_at)
-    grad_qkv, sends = held(grad_qkv, up_cuts + tuple(down_blocks))
-    up_cuts, down_blocks = sends[:seq_size], sends[seq_size:]
-    up_blocks = [up_cuts[0]] + [swap(up_cuts[k], "seq", k, seq_size) for k in range(1, seq_size)]
     part_normed = apply_back(grad_qkv, qkv_pair)
     grad_norm1_gain = jnp.sum(part_normed * unit_all, axis=0)
     grad_norm1_bias = jnp.sum(part_normed, axis=0)
@@ -623,12 +613,12 @@
     plain = [by_device(v) for v in (grad_qv_bias, grad_out_bias, grad_up_bias, grad_down_bias)]
     moved = [by_device(v) for v in (grad_norm1_gain, grad_norm1_bias, grad_norm2_gain, grad_norm2_bias)]
     spare = [jnp.zeros((dp_size, seq_size, 1), f32)] * 2
-    plain_x = slotted(spare + plain[:2] + spare + plain[2:])
+    counts = jnp.broadcast_to(counted, (dp_size, seq_size, 6))
+    plain_x = slotted(spare + plain[:2] + spare + plain[2:] + [counts])
     plain_x = pick_rows(plain_x.reshape(dp_size, -1), index_of(to_x)).reshape(plain_x.shape)
     spare = spare[:1] * 2
-    counts = jnp.broadcast_to(counted, (dp_size, seq_size, 6))
-    vec_grads = plain_x + slotted(moved[:2] + spare + moved[2:] + spare + [counts])
-    vec_grads = vec_grads.astype(bf16).reshape(2, -1, 128)
+    vec_grads = plain_x + slotted(moved[:2] + spare + moved[2:] + spare + spare[:1])
+    vec_grads = whole_rows(vec_grads.astype(bf16)).reshape(2, -1, 128)
     qkv_grads = weight_grads(normed_one, grad_qkv)
     one_sum = collect(
         [qkv_grads[0], vec_grads[0], out_grads[0]],
@@ -637,19 +627,25 @@
         False,
     )
     odd = next(one_sum)
-    part_normed, beside = held(part_normed, (odd[0], odd[2]) + tuple(up_blocks))
-    up_blocks = beside[2:]
+    part_normed, beside = held(
+        part_normed, (odd[0], odd[2]) + tuple(up_sends) + tuple(down_blocks)
+    )
+    up_cuts = seq_cuts(up_sum.send(beside[2:4])[0], seq_size, seq_at)
+    down_blocks = beside[4:]
     sends = run(one_sum, (beside[0], odd[1], beside[1]), far + 1)
     one_cuts = seq_cuts(sends[0], seq_size, seq_at)
     parts = [cut_rows(part_normed, 0)]
     parts += [swap(cut_rows(part_normed, k), "seq", k, seq_size) for k in range(1, seq_size)]
-    parts[1], one_cuts = held(parts[1], one_cuts)
+    parts[1], beside = held(parts[1], one_cuts + up_cuts)
+    one_cuts, up_cuts = beside[:seq_size], beside[seq_size:]
+    up_blocks = [up_cuts[0]] + [swap(up_cuts[k], "seq", k, seq_size) for k in range(1, seq_size)]
     one_blocks = [one_cuts[0]]
     one_blocks += [swap(one_cuts[k], "seq", k, seq_size) for k in range(1, seq_size)]
     grad_normed_one = sum(part.astype(f32) for part in parts)
     unit_one, inverse_one = layer_norm_parts(own_x.astype(f32), gain_one, shift_one)[1:]
     grad_in_norm = layer_norm_back(grad_normed_one, unit_one, inverse_one, gain_one)[0]
     tokens_grad = (grad_middle + pick_columns(grad_in_norm, *from_x)).astype(bf16)[None]
+    tokens_grad, up_blocks = held(tokens_grad, up_blocks)
     up_grad = sum(block.astype(f32) for block in up_blocks)
     down_grad = sum(block.astype(f32) for block in down_blocks)
     one_blocks = [block.astype(f32) for block in one_blocks]

time: 452 us -> 449 us (level)
  waiting for transfers between devices: 122 us -> 101 us
  other arithmetic: 86.8 us -> 92.5 us
  matrix products: 57.7 us -> 62.4 us
    ppermute x58, waiting for transfers between devices: 122 us -> 101 us  [swap(): return lax.ppermute(value, axis, [(i, i ^ bit) for i in range(size)])]
  transfers between devices with their start and end apart: 58 -> 58, of which waited for: 25 -> 19; matrix products, arithmetic and copies ran while one was open for 28% -> 32% of each run, Pallas kernels for 12% -> 12%
where the time goes in v1:
time: 449 us; the launch traced here: 441 us
  waiting for transfers between devices  101 us (22%)
  other arithmetic  92.5 us (21%)
  starting transfers between devices  84.3 us (19%)
  Pallas kernels  64.4 us (14%)
  matrix products  62.4 us (14%)
  local copies, waits for them, and re-layouts  32.3 us (7%)
    ppermute x58, waiting for transfers between devices, swap(): return lax.ppermute(value, axis, [(i, i ^ bit) for i in range(size)])  101 us
    ppermute x58, starting transfers between devices, swap(): return lax.ppermute(value, axis, [(i, i ^ bit) for i in range(size)])  84.3 us
    dot_general x8, matrix products, dot_rows(): jnp.einsum('rk,rn->kn', rows, grad, preferred_element_type=jnp.float32)  22.6 us
    dot_general x8, matrix products, dot(): return jnp.dot(left, right, preferred_element_type=jnp.float32)  22 us
    pallas_call x8, Pallas kernels, pick_columns(): pl.pallas_call(functools.partial(pick_columns_body, table), out_shape=jax...  20.7 us
    pallas_call x1, Pallas kernels, attend_back(): pl.pallas_call(attend_back_body, grid=(length // block,), in_specs=info_s...  19.5 us
    dot_general x8, matrix products, dot_back(): jnp.einsum('rn,kn->rk', grad, weight, preferred_element_type=jnp.float32)  17.8 us
    pallas_call x1, Pallas kernels, attend(): pl.pallas_call(attend_body, grid=(length // block,), in_specs=info_specs...  16 us
  transfers between devices with their start and end apart: 58, of which 19 were waited for; matrix products, arithmetic and copies ran while one was open for 32% of the time, Pallas kernels for 12%

profile of v1, /device:TPU:0, one launch (start us, length us, event | category | flops | bytes accessed | tf_op | source)
XLA Modules:
  0.0 440.9 jit_solution(6906931394765619827)
XLA Ops:
  2.5 3.1 collective-permute-start.1
  25.5 3.0 collective-permute-done
  28.5 3.5 collective-permute-start.3
  32.6 9.0 %collective-permute-done.3 = bf16[32,896]{1,0:T(8,128)(2,1)S(1)} collective-permute-done((bf16[32,896]{1,0:T(8,128)(2,1)S(1)}, bf16[32,896]{1,0:T(8,128)(2,1)S(1)}, u32[]{:S(2)}, u32[]{:S(2)}) %collective-permute-start.3) | collective-permute-done | bytes 57376 | tf_op jit(solution)/shard_map/ppermute | solution.py:53
  43.3 3.2 collective-permute-start.5
  50.3 12.0 %collective-permute-done.9 = bf16[64,5120]{1,0:T(8,128)(2,1)S(1)} collective-permute-done((bf16[64,5120]{1,0:T(8,128)(2,1)S(1)}, bf16[64,5120]{1,0:T(8,128)(2,1)S(1)}, u32[]{:S(2)}, u32[]{:S(2)}) %collective-permute-start.9) | collective-permute-done | bytes 655392 | tf_op jit(solution)/shard_map/ppermute | solution.py:53
  65.7 16.3 %collective-permute-done.5 = bf16[256,1024]{1,0:T(8,128)(2,1)S(1)} collective-permute-done((bf16[256,1024]{1,0:T(8,128)(2,1)}, bf16[256,1024]{1,0:T(8,128)(2,1)S(1)}, u32[]{:S(2)}, u32[]{:S(2)}) %collective-permute-start.5) | collective-permute-done | bytes 524320 | tf_op jit(solution)/shard_map/ppermute | solution.py:53
  82.0 9.3 %collective-permute-start.14 = (bf16[128,1024]{1,0:T(8,128)(2,1)}, bf16[128,1024]{1,0:T(8,128)(2,1)}, u32[]{:S(2)}, u32[]{:S(2)}) collective-permute-start(bf16[128,1024]{1,0:T(8,128)(2,1)} %param.34), channel_id=1, source_target_pairs={{0,1},{1,0},{2,3},{3,2},{4,5},{5,4},{6,7},{7,6},{8,9},{9,8},{10,11... | collective-permute-start | bytes 786440 | tf_op jit(solution)/shard_map/ppermute | solution.py:53
  105.1 3.1 fusion.6
  111.8 16.0 %attend.1 = (bf16[1024,256]{1,0:T(8,128)(2,1)}, f32[1024,4]{1,0:T(8,128)}) custom-call(s32[1]{0:T(128)} %copy.132.valid_ref, s32[1024,3]{1,0:T(8,128)} %copy.97.query_ref, s32[3,1024]{1,0:T(4,128)} %pad_add_fusion.key_ref, bf16[1024,768]{1,0:T(8,128)(2,1)} %add_convert_fusion.q_ref.k_ref.v_ref, bf16[1024,768]{1,0:T(8,128)(2,1)} %add_convert_fusion.q_ref.k_ref.v_ref, ...), custom_call_target="tpu_custom_call" | custom-call | flops 4294967296 | bytes 8388608 | tf_op jit(solution)/shard_map/attend/pallas_call | solution.py:366
  127.9 2.5 collective-permute-done.18.refs_3_
  130.4 4.6 %place_rows.2 = bf16[512,5120]{1,0:T(8,128)(2,1)} custom-call(bf16[128,5120]{1,0:T(8,128)(2,1)} %copy-done.19, bf16[128,5120]{1,0:T(8,128)(2,1)} %pad_maximum_fusion.3.refs_1_, bf16[128,5120]{1,0:T(8,128)(2,1)} %collective-permute-done.17.refs_2_, bf16[128,5120]{1,0:T(8,128)(2,1)} %collective-permute-done.18.refs_3_), custom_call_target="tpu_custom_call" | custom-call | bytes 10485760 | tf_op jit(solution)/shard_map/place_rows/pallas_call | solution.py:142
  141.5 3.6 collective-permute-done.21
  145.1 4.8 %collective-permute-start.19 = (bf16[256,256]{1,0:T(8,128)(2,1)S(1)}, bf16[256,256]{1,0:T(8,128)(2,1)S(1)}, u32[]{:S(2)}, u32[]{:S(2)}) collective-permute-start(bf16[256,256]{1,0:T(8,128)(2,1)S(1)} %get-tuple-element.269), channel_id=1, source_target_pairs={{0,1},{1,0},{2,3},{3,2},{4,5},{5,4},{6,7},{7,6},{8,9},{9,8},{10,11... | collective-permute-start | bytes 393224 | tf_op jit(solution)/shard_map/ppermute | solution.py:53
  151.8 2.7 collective-permute-done.19
  163.8 3.1 convert_add_fusion.1
  173.5 3.6 fusion.26
  177.2 5.5 %fusion.in_ref = f32[256,4096]{1,0:T(8,128)} fusion(f32[256,4096]{1,0:T(8,128)S(1)} %fusion.26, bf16[512,5120]{1,0:T(8,128)(2,1)} %collective-permute-done.24, f32[4096]{0:T(1024)S(1)} %bitcast.185, bf16[256,1024]{1,0:T(8,128)(2,1)S(1)} %add_convert_fusion.30), kind=kOutput, calls=%fused_computation.6 | convolution fusion | flops 1075838976 | bytes 12861440 | tf_op jit(solution)/shard_map/dot_general | solution.py:248
  182.6 4.5 %pick_columns.11 = f32[256,4096]{1,0:T(8,128)} custom-call(s32[1]{0:T(128)} %bitcast.6.flip_ref, f32[256,4096]{1,0:T(8,128)} %fusion.in_ref), custom_call_target="tpu_custom_call" | custom-call | tf_op jit(solution)/shard_map/pick_columns/pallas_call | solution.py:97
  187.2 3.5 fusion.13
  190.6 3.4 convolution_convert_fusion.3
  194.0 3.6 place_rows.3
  204.4 2.6 add_convert_fusion.27
  209.3 3.9 fusion.124
  213.2 3.7 fusion.20.in_ref
  216.9 3.2 pick_columns.12
  220.0 5.2 %convolution_convert_fusion.1 = bf16[512,4096]{1,0:T(8,128)(2,1)} fusion(bf16[256,4096]{1,0:T(8,128)(2,1)} %pick_columns.12, bf16[256,1024]{1,0:T(8,128)(2,1)} %copy-done.20), kind=kOutput, calls=%fused_computation.4 | convolution fusion | flops 1075838976 | bytes 6553600 | tf_op jit(solution)/shard_map/rk,rn->kn/dot_general | solution.py:256
  225.2 3.5 fusion.24
  228.7 3.6 fusion.21
  247.4 2.8 collective-permute-start.31
  253.2 2.6 convolution_convert_fusion.5
  255.8 4.2 convolution_convert_fusion
  260.0 3.6 fusion.47
  272.9 4.2 fusion.110
  280.1 2.6 collective-permute-done.29
  284.4 3.8 add_convert_fusion.22
  296.9 19.5 %attend_back.1 = bf16[1024,768]{1,0:T(8,128)(2,1)} custom-call(s32[1]{0:T(128)} %copy.132.valid_ref, s32[1024,3]{1,0:T(8,128)} %copy.97.query_ref, s32[3,1024]{1,0:T(4,128)} %pad_add_fusion.key_ref, f32[1024,4]{1,0:T(8,128)} %get-tuple-element.137.lse_ref, bf16[1024,768]{1,0:T(8,128)(2,1)} %add_convert_fusion.q_ref.k_ref.v_ref, ...), custom_call_target="tpu_custom_call" | custom-call | flops 10737418240 | bytes 16777216 | tf_op jit(solution)/shard_map/attend_back/pallas_call | solution.py:390
  316.4 3.0 fusion.68
  333.6 2.5 fusion.29
  336.1 3.5 convolution_convert_fusion.7
  339.7 3.4 add_convert_fusion.8
  355.0 2.9 collective-permute-start.50
  362.1 14.9 %collective-permute-done.46 = bf16[2,128,1920]{2,1,0:T(8,128)(2,1)} collective-permute-done((bf16[2,128,1920]{2,1,0:T(8,128)(2,1)}, bf16[2,128,1920]{2,1,0:T(8,128)(2,1)}, u32[]{:S(2)}, u32[]{:S(2)}) %collective-permute-start.46) | collective-permute-done | bytes 983072 | tf_op jit(solution)/shard_map/ppermute | solution.py:53
  377.0 3.4 collective-permute-start.42
  381.6 5.7 %collective-permute-done.49 = bf16[1,64,4096]{2,1,0:T(8,128)(2,1)S(1)} collective-permute-done((bf16[1,64,4096]{2,1,0:T(8,128)(2,1)}, bf16[1,64,4096]{2,1,0:T(8,128)(2,1)S(1)}, u32[]{:S(2)}, u32[]{:S(2)}) %collective-permute-start.49) | collective-permute-done | bytes 524320 | tf_op jit(solution)/shard_map/ppermute | solution.py:53
  391.7 7.9 %collective-permute-done.47 = bf16[1,128,1920]{2,1,0:T(8,128)(2,1)S(1)} collective-permute-done((bf16[1,128,1920]{2,1,0:T(8,128)(2,1)S(1)}, bf16[1,128,1920]{2,1,0:T(8,128)(2,1)S(1)}, u32[]{:S(2)}, u32[]{:S(2)}) %collective-permute-start.47) | collective-permute-done | bytes 491552 | tf_op jit(solution)/shard_map/ppermute | solution.py:53
  418.8 4.1 collective-permute-done.56
  430.0 9.8 %collective-permute-done.53 = bf16[32,4096]{1,0:T(8,128)(2,1)S(1)} collective-permute-done((bf16[32,4096]{1,0:T(8,128)(2,1)}, bf16[32,4096]{1,0:T(8,128)(2,1)S(1)}, u32[]{:S(2)}, u32[]{:S(2)}) %collective-permute-start.53) | collective-permute-done | bytes 262176 | tf_op jit(solution)/shard_map/ppermute | solution.py:53
  (414 shorter events, 183.1 us)
Async XLA Ops:
  2.5 30.1 %collective-permute-start.1 = (bf16[32,5120]{1,0:T(8,128)(2,1)S(1)}, bf16[32,5120]{1,0:T(8,128)(2,1)S(1)}, u32[]{:S(2)}, u32[]{:S(2)}) collective-permute-start(bf16[32,5120]{1,0:T(8,128)(2,1)S(1)} %constant_dynamic-update-slice_fusion), channel_id=1, source_target_pairs={{0,1},{1,0},{2,3},{3,2},{4,5},{5,4},{6,7},{7,6},{8,9},{9,8},{10,11... | collective-permute-start | bytes 983048 | tf_op jit(solution)/shard_map/ppermute | solution.py:53
  5.6 27.0 %collective-permute-start.7 = (bf16[32,5120]{1,0:T(8,128)(2,1)S(1)}, bf16[32,5120]{1,0:T(8,128)(2,1)S(1)}, u32[]{:S(2)}, u32[]{:S(2)}) collective-permute-start(bf16[32,5120]{1,0:T(8,128)(2,1)S(1)} %constant_dynamic-update-slice_fusion), channel_id=1, source_target_pairs={{0,3},{1,2},{2,1},{3,0},{4,7},{5,6},{6,5},{7,4},{8,11},{9,10},{10,... | collective-permute-start | bytes 983048 | tf_op jit(solution)/shard_map/ppermute | solution.py:53
  8.1 33.5 %collective-permute-start.4 = (bf16[32,5120]{1,0:T(8,128)(2,1)S(1)}, bf16[32,5120]{1,0:T(8,128)(2,1)S(1)}, u32[]{:S(2)}, u32[]{:S(2)}) collective-permute-start(bf16[32,5120]{1,0:T(8,128)(2,1)S(1)} %constant_dynamic-update-slice_fusion), channel_id=1, source_target_pairs={{0,2},{1,3},{2,0},{3,1},{4,6},{5,7},{6,4},{7,5},{8,10},{9,11},{10,... | collective-permute-start | bytes 983048 | tf_op jit(solution)/shard_map/ppermute | solution.py:53
  14.0 14.5 %collective-permute-start = (bf16[32,896]{1,0:T(8,128)(2,1)S(1)}, bf16[32,896]{1,0:T(8,128)(2,1)S(1)}, u32[]{:S(2)}, u32[]{:S(2)}) collective-permute-start(bf16[32,896]{1,0:T(8,128)(2,1)S(1)} %get-tuple-element.301), channel_id=1, source_target_pairs={{0,1},{1,0},{2,3},{3,2},{4,5},{5,4},{6,7},{7,6},{8,9},{9,8},{10,11... | collective-permute-start | bytes 172040 | tf_op jit(solution)/shard_map/ppermute | solution.py:53
  15.9 16.7 %collective-permute-start.6 = (bf16[32,896]{1,0:T(8,128)(2,1)S(1)}, bf16[32,896]{1,0:T(8,128)(2,1)S(1)}, u32[]{:S(2)}, u32[]{:S(2)}) collective-permute-start(bf16[32,896]{1,0:T(8,128)(2,1)S(1)} %get-tuple-element.300), channel_id=1, source_target_pairs={{0,3},{1,2},{2,1},{3,0},{4,7},{5,6},{6,5},{7,4},{8,11},{9,10},{10,... | collective-permute-start | bytes 172040 | tf_op jit(solution)/shard_map/ppermute | solution.py:53
  28.5 13.1 %collective-permute-start.3 = (bf16[32,896]{1,0:T(8,128)(2,1)S(1)}, bf16[32,896]{1,0:T(8,128)(2,1)S(1)}, u32[]{:S(2)}, u32[]{:S(2)}) collective-permute-start(bf16[32,896]{1,0:T(8,128)(2,1)S(1)} %get-tuple-element.302), channel_id=1, source_target_pairs={{0,2},{1,3},{2,0},{3,1},{4,6},{5,7},{6,4},{7,5},{8,10},{9,11},{10,... | collective-permute-start | bytes 172040 | tf_op jit(solution)/shard_map/ppermute | solution.py:53
  43.3 22.4 %collective-permute-start.2 = (bf16[256,1024]{1,0:T(8,128)(2,1)}, bf16[256,1024]{1,0:T(8,128)(2,1)S(1)}, u32[]{:S(2)}, u32[]{:S(2)}) collective-permute-start(bf16[256,1024]{1,0:T(8,128)(2,1)} %pick_columns.8), channel_id=1, source_target_pairs={{0,1},{1,0},{2,3},{3,2},{4,5},{5,4},{6,7},{7,6},{8,9},{9,8},{10,11... | collective-permute-start | bytes 1572872 | tf_op jit(solution)/shard_map/ppermute | solution.py:53
  43.3 38.7 %collective-permute-start.5 = (bf16[256,1024]{1,0:T(8,128)(2,1)}, bf16[256,1024]{1,0:T(8,128)(2,1)S(1)}, u32[]{:S(2)}, u32[]{:S(2)}) collective-permute-start(bf16[256,1024]{1,0:T(8,128)(2,1)} %pick_columns.8), channel_id=1, source_target_pairs={{0,2},{1,3},{2,0},{3,1},{4,6},{5,7},{6,4},{7,5},{8,10},{9,11},{10,... | collective-permute-start | bytes 1572872 | tf_op jit(solution)/shard_map/ppermute | solution.py:53
  46.6 35.5 %collective-permute-start.8 = (bf16[256,1024]{1,0:T(8,128)(2,1)}, bf16[256,1024]{1,0:T(8,128)(2,1)S(1)}, u32[]{:S(2)}, u32[]{:S(2)}) collective-permute-start(bf16[256,1024]{1,0:T(8,128)(2,1)} %pick_columns.8), channel_id=1, source_target_pairs={{0,3},{1,2},{2,1},{3,0},{4,7},{5,6},{6,5},{7,4},{8,11},{9,10},{10,... | collective-permute-start | bytes 1572872 | tf_op jit(solution)/shard_map/ppermute | solution.py:53
  47.9 14.4 %collective-permute-start.9 = (bf16[64,5120]{1,0:T(8,128)(2,1)S(1)}, bf16[64,5120]{1,0:T(8,128)(2,1)S(1)}, u32[]{:S(2)}, u32[]{:S(2)}) collective-permute-start(bf16[64,5120]{1,0:T(8,128)(2,1)S(1)} %pad_maximum_fusion.13), channel_id=1, source_target_pairs={{0,8},{4,12},{8,0},{12,4},{16,24},{20,28},{24,16},{28,20},{1,9},{5... | collective-permute-start | bytes 1966088 | tf_op jit(solution)/shard_map/ppermute | solution.py:53
  48.6 15.3 %collective-permute-start.10 = (bf16[64,5120]{1,0:T(8,128)(2,1)S(1)}, bf16[64,5120]{1,0:T(8,128)(2,1)S(1)}, u32[]{:S(2)}, u32[]{:S(2)}) collective-permute-start(bf16[64,5120]{1,0:T(8,128)(2,1)S(1)} %pad_maximum_fusion.14), channel_id=1, source_target_pairs={{0,16},{4,20},{8,24},{12,28},{16,0},{20,4},{24,8},{28,12},{1,17},{... | collective-permute-start | bytes 1966088 | tf_op jit(solution)/shard_map/ppermute | solution.py:53
  62.3 33.0 %collective-permute-start.12 = (bf16[256,896]{1,0:T(8,128)(2,1)S(1)}, bf16[256,896]{1,0:T(8,128)(2,1)S(1)}, u32[]{:S(2)}, u32[]{:S(2)}) collective-permute-start(bf16[256,896]{1,0:T(8,128)(2,1)S(1)} %get-tuple-element.274), channel_id=1, source_target_pairs={{0,16},{4,20},{8,24},{12,28},{16,0},{20,4},{24,8},{28,12},{1,17},{... | collective-permute-start | bytes 1376264 | tf_op jit(solution)/shard_map/ppermute | solution.py:53
  82.0 45.8 %collective-permute-start.14 = (bf16[128,1024]{1,0:T(8,128)(2,1)}, bf16[128,1024]{1,0:T(8,128)(2,1)}, u32[]{:S(2)}, u32[]{:S(2)}) collective-permute-start(bf16[128,1024]{1,0:T(8,128)(2,1)} %param.34), channel_id=1, source_target_pairs={{0,1},{1,0},{2,3},{3,2},{4,5},{5,4},{6,7},{7,6},{8,9},{9,8},{10,11... | collective-permute-start | bytes 786440 | tf_op jit(solution)/shard_map/ppermute | solution.py:53
  91.3 36.5 %collective-permute-start.15 = (bf16[128,1024]{1,0:T(8,128)(2,1)}, bf16[128,1024]{1,0:T(8,128)(2,1)}, u32[]{:S(2)}, u32[]{:S(2)}) collective-permute-start(bf16[128,1024]{1,0:T(8,128)(2,1)} %param.34), channel_id=1, source_target_pairs={{0,2},{1,3},{2,0},{3,1},{4,6},{5,7},{6,4},{7,5},{8,10},{9,11},{10,... | collective-permute-start | bytes 786440 | tf_op jit(solution)/shard_map/ppermute | solution.py:53
  92.2 35.7 %collective-permute-start.16 = (bf16[128,1024]{1,0:T(8,128)(2,1)}, bf16[128,1024]{1,0:T(8,128)(2,1)}, u32[]{:S(2)}, u32[]{:S(2)}) collective-permute-start(bf16[128,1024]{1,0:T(8,128)(2,1)} %param.34), channel_id=1, source_target_pairs={{0,3},{1,2},{2,1},{3,0},{4,7},{5,6},{6,5},{7,4},{8,11},{9,10},{10,... | collective-permute-start | bytes 786440 | tf_op jit(solution)/shard_map/ppermute | solution.py:53
  93.7 34.2 %collective-permute-start.17 = (bf16[128,5120]{1,0:T(8,128)(2,1)S(1)}, bf16[128,5120]{1,0:T(8,128)(2,1)}, u32[]{:S(2)}, u32[]{:S(2)}) collective-permute-start(bf16[128,5120]{1,0:T(8,128)(2,1)S(1)} %pad_maximum_fusion.2.refs_0_), channel_id=1, source_target_pairs={{0,16},{4,20},{8,24},{12,28},{16,0},{20,4},{24,8},{28,12},{1,17},{... | collective-permute-start | bytes 3932168 | tf_op jit(solution)/shard_map/ppermute | solution.py:53
  98.9 31.6 %collective-permute-start.18 = (bf16[128,5120]{1,0:T(8,128)(2,1)}, bf16[128,5120]{1,0:T(8,128)(2,1)}, u32[]{:S(2)}, u32[]{:S(2)}) collective-permute-start(bf16[128,5120]{1,0:T(8,128)(2,1)} %pad_maximum_fusion.3.refs_1_), channel_id=1, source_target_pairs={{0,8},{4,12},{8,0},{12,4},{16,24},{20,28},{24,16},{28,20},{1,9},{5... | collective-permute-start | bytes 3932168 | tf_op jit(solution)/shard_map/ppermute | solution.py:53
  136.6 27.2 %collective-permute-start.24 = (bf16[512,5120]{1,0:T(8,128)(2,1)}, bf16[512,5120]{1,0:T(8,128)(2,1)}, u32[]{:S(2)}, u32[]{:S(2)}) collective-permute-start(bf16[512,5120]{1,0:T(8,128)(2,1)} %place_rows.2), channel_id=1, source_target_pairs={{0,4},{4,0},{8,12},{12,8},{16,20},{20,16},{24,28},{28,24},{1,5},{5... | collective-permute-start | bytes 15728648 | tf_op jit(solution)/shard_map/ppermute | solution.py:53
  139.2 16.1 %collective-permute-start.22 = (bf16[256,1024]{1,0:T(8,128)(2,1)S(1)}, bf16[256,1024]{1,0:T(8,128)(2,1)}, u32[]{:S(2)}, u32[]{:S(2)}) collective-permute-start(bf16[256,1024]{1,0:T(8,128)(2,1)S(1)} %get-tuple-element.253), channel_id=1, source_target_pairs={{0,8},{4,12},{8,0},{12,4},{16,24},{20,28},{24,16},{28,20},{1,9},{5... | collective-permute-start | bytes 1572872 | tf_op jit(solution)/shard_map/ppermute | solution.py:53
  139.8 17.6 %collective-permute-start.23 = (bf16[256,1024]{1,0:T(8,128)(2,1)S(1)}, bf16[256,1024]{1,0:T(8,128)(2,1)}, u32[]{:S(2)}, u32[]{:S(2)}) collective-permute-start(bf16[256,1024]{1,0:T(8,128)(2,1)S(1)} %get-tuple-element.252), channel_id=1, source_target_pairs={{0,16},{4,20},{8,24},{12,28},{16,0},{20,4},{24,8},{28,12},{1,17},{... | collective-permute-start | bytes 1572872 | tf_op jit(solution)/shard_map/ppermute | solution.py:53
  141.2 10.5 %collective-permute-start.20 = (bf16[256,256]{1,0:T(8,128)(2,1)S(1)}, bf16[256,256]{1,0:T(8,128)(2,1)S(1)}, u32[]{:S(2)}, u32[]{:S(2)}) collective-permute-start(bf16[256,256]{1,0:T(8,128)(2,1)S(1)} %get-tuple-element.268), channel_id=1, source_target_pairs={{0,2},{1,3},{2,0},{3,1},{4,6},{5,7},{6,4},{7,5},{8,10},{9,11},{10,... | collective-permute-start | bytes 393224 | tf_op jit(solution)/shard_map/ppermute | solution.py:53
  159.5 27.6 %collective-permute-start.25 = (bf16[512,1024]{1,0:T(8,128)(2,1)}, bf16[512,1024]{1,0:T(8,128)(2,1)}, u32[]{:S(2)}, u32[]{:S(2)}) collective-permute-start(bf16[512,1024]{1,0:T(8,128)(2,1)} %pad_maximum_fusion.5.refs_0_), channel_id=1, source_target_pairs={{0,16},{4,20},{8,24},{12,28},{16,0},{20,4},{24,8},{28,12},{1,17},{... | collective-permute-start | bytes 3145736 | tf_op jit(solution)/shard_map/ppermute | solution.py:53
  160.0 27.1 %collective-permute-start.26 = (bf16[512,1024]{1,0:T(8,128)(2,1)}, bf16[512,1024]{1,0:T(8,128)(2,1)}, u32[]{:S(2)}, u32[]{:S(2)}) collective-permute-start(bf16[512,1024]{1,0:T(8,128)(2,1)} %pad_maximum_fusion.6.refs_1_), channel_id=1, source_target_pairs={{0,8},{4,12},{8,0},{12,4},{16,24},{20,28},{24,16},{28,20},{1,9},{5... | collective-permute-start | bytes 3145736 | tf_op jit(solution)/shard_map/ppermute | solution.py:53
  197.6 11.7 %collective-permute-start.27 = (bf16[2048,1024]{1,0:T(8,128)(2,1)}, bf16[2048,1024]{1,0:T(8,128)(2,1)}, u32[]{:S(2)}, u32[]{:S(2)}) collective-permute-start(bf16[2048,1024]{1,0:T(8,128)(2,1)} %place_rows.3), channel_id=1, source_target_pairs={{0,4},{4,0},{8,12},{12,8},{16,20},{20,16},{24,28},{28,24},{1,5},{5... | collective-permute-start | bytes 12582920 | tf_op jit(solution)/shard_map/ppermute | solution.py:53
  233.4 54.9 %collective-permute-start.34 = (bf16[512,4096]{1,0:T(8,128)(2,1)}, bf16[512,4096]{1,0:T(8,128)(2,1)}, u32[]{:S(2)}, u32[]{:S(2)}) collective-permute-start(bf16[512,4096]{1,0:T(8,128)(2,1)} %convolution_convert_fusion.1), channel_id=1, source_target_pairs={{0,4},{4,0},{8,12},{12,8},{16,20},{20,16},{24,28},{28,24},{1,5},{5... | collective-permute-start | bytes 12582920 | tf_op jit(solution)/shard_map/ppermute | solution.py:53
  247.4 30.3 %collective-permute-start.31 = (bf16[256,256]{1,0:T(8,128)(2,1)}, bf16[256,256]{1,0:T(8,128)(2,1)S(1)}, u32[]{:S(2)}, u32[]{:S(2)}) collective-permute-start(bf16[256,256]{1,0:T(8,128)(2,1)} %get-tuple-element.263), channel_id=1, source_target_pairs={{0,3},{1,2},{2,1},{3,0},{4,7},{5,6},{6,5},{7,4},{8,11},{9,10},{10,... | collective-permute-start | bytes 393224 | tf_op jit(solution)/shard_map/ppermute | solution.py:53
  250.2 34.2 %collective-permute-start.33 = (bf16[2,256,1024]{2,1,0:T(8,128)(2,1)}, bf16[2,256,1024]{2,1,0:T(8,128)(2,1)}, u32[]{:S(2)}, u32[]{:S(2)}) collective-permute-start(bf16[2,256,1024]{2,1,0:T(8,128)(2,1)} %pad_maximum_fusion.8), channel_id=1, source_target_pairs={{0,8},{4,12},{8,0},{12,4},{16,24},{20,28},{24,16},{28,20},{1,9},{5... | collective-permute-start | bytes 3145736 | tf_op jit(solution)/shard_map/ppermute | solution.py:53
  251.7 32.8 %collective-permute-start.32 = (bf16[2,256,1024]{2,1,0:T(8,128)(2,1)}, bf16[2,256,1024]{2,1,0:T(8,128)(2,1)}, u32[]{:S(2)}, u32[]{:S(2)}) collective-permute-start(bf16[2,256,1024]{2,1,0:T(8,128)(2,1)} %pad_maximum_fusion.7), channel_id=1, source_target_pairs={{0,16},{4,20},{8,24},{12,28},{16,0},{20,4},{24,8},{28,12},{1,17},{... | collective-permute-start | bytes 3145736 | tf_op jit(solution)/shard_map/ppermute | solution.py:53
  268.9 11.2 %collective-permute-start.30 = (bf16[256,256]{1,0:T(8,128)(2,1)}, bf16[256,256]{1,0:T(8,128)(2,1)}, u32[]{:S(2)}, u32[]{:S(2)}) collective-permute-start(bf16[256,256]{1,0:T(8,128)(2,1)} %get-tuple-element.264), channel_id=1, source_target_pairs={{0,2},{1,3},{2,0},{3,1},{4,6},{5,7},{6,4},{7,5},{8,10},{9,11},{10,... | collective-permute-start | bytes 393224 | tf_op jit(solution)/shard_map/ppermute | solution.py:53
  292.8 23.6 %collective-permute-start.36 = (bf16[1,256,1024]{2,1,0:T(8,128)(2,1)}, bf16[1,256,1024]{2,1,0:T(8,128)(2,1)S(1)}, u32[]{:S(2)}, u32[]{:S(2)}) collective-permute-start(bf16[1,256,1024]{2,1,0:T(8,128)(2,1)} %get-tuple-element.144), channel_id=1, source_target_pairs={{0,16},{4,20},{8,24},{12,28},{16,0},{20,4},{24,8},{28,12},{1,17},{... | collective-permute-start | bytes 1572872 | tf_op jit(solution)/shard_map/ppermute | solution.py:53
  293.3 23.1 %collective-permute-start.35 = (bf16[1,256,1024]{2,1,0:T(8,128)(2,1)}, bf16[1,256,1024]{2,1,0:T(8,128)(2,1)}, u32[]{:S(2)}, u32[]{:S(2)}) collective-permute-start(bf16[1,256,1024]{2,1,0:T(8,128)(2,1)} %get-tuple-element.143), channel_id=1, source_target_pairs={{0,8},{4,12},{8,0},{12,4},{16,24},{20,28},{24,16},{28,20},{1,9},{5... | collective-permute-start | bytes 1572872 | tf_op jit(solution)/shard_map/ppermute | solution.py:53
  293.8 45.9 %collective-permute-start.38 = (bf16[2,64,4096]{2,1,0:T(8,128)(2,1)}, bf16[2,64,4096]{2,1,0:T(8,128)(2,1)}, u32[]{:S(2)}, u32[]{:S(2)}) collective-permute-start(bf16[2,64,4096]{2,1,0:T(8,128)(2,1)} %pad_maximum_fusion.11), channel_id=1, source_target_pairs={{0,8},{4,12},{8,0},{12,4},{16,24},{20,28},{24,16},{28,20},{1,9},{5... | collective-permute-start | bytes 3145736 | tf_op jit(solution)/shard_map/ppermute | solution.py:53
  295.3 44.3 %collective-permute-start.37 = (bf16[2,64,4096]{2,1,0:T(8,128)(2,1)}, bf16[2,64,4096]{2,1,0:T(8,128)(2,1)}, u32[]{:S(2)}, u32[]{:S(2)}) collective-permute-start(bf16[2,64,4096]{2,1,0:T(8,128)(2,1)} %pad_maximum_fusion.10), channel_id=1, source_target_pairs={{0,16},{4,20},{8,24},{12,28},{16,0},{20,4},{24,8},{28,12},{1,17},{... | collective-permute-start | bytes 3145736 | tf_op jit(solution)/shard_map/ppermute | solution.py:53
  322.5 20.6 %collective-permute-start.39 = (bf16[128,1024]{1,0:T(8,128)(2,1)}, bf16[128,1024]{1,0:T(8,128)(2,1)}, u32[]{:S(2)}, u32[]{:S(2)}) collective-permute-start(bf16[128,1024]{1,0:T(8,128)(2,1)} %get-tuple-element.149), channel_id=1, source_target_pairs={{0,1},{1,0},{2,3},{3,2},{4,5},{5,4},{6,7},{7,6},{8,9},{9,8},{10,11... | collective-permute-start | bytes 786440 | tf_op jit(solution)/shard_map/ppermute | solution.py:53
  324.5 20.3 %collective-permute-start.40 = (bf16[128,1024]{1,0:T(8,128)(2,1)}, bf16[128,1024]{1,0:T(8,128)(2,1)}, u32[]{:S(2)}, u32[]{:S(2)}) collective-permute-start(bf16[128,1024]{1,0:T(8,128)(2,1)} %get-tuple-element.150), channel_id=1, source_target_pairs={{0,2},{1,3},{2,0},{3,1},{4,6},{5,7},{6,4},{7,5},{8,10},{9,11},{10,... | collective-permute-start | bytes 786440 | tf_op jit(solution)/shard_map/ppermute | solution.py:53
  325.5 19.3 %collective-permute-start.41 = (bf16[128,1024]{1,0:T(8,128)(2,1)}, bf16[128,1024]{1,0:T(8,128)(2,1)}, u32[]{:S(2)}, u32[]{:S(2)}) collective-permute-start(bf16[128,1024]{1,0:T(8,128)(2,1)} %get-tuple-element.151), channel_id=1, source_target_pairs={{0,3},{1,2},{2,1},{3,0},{4,7},{5,6},{6,5},{7,4},{8,11},{9,10},{10,... | collective-permute-start | bytes 786440 | tf_op jit(solution)/shard_map/ppermute | solution.py:53
  352.0 24.9 %collective-permute-start.46 = (bf16[2,128,1920]{2,1,0:T(8,128)(2,1)}, bf16[2,128,1920]{2,1,0:T(8,128)(2,1)}, u32[]{:S(2)}, u32[]{:S(2)}) collective-permute-start(bf16[2,128,1920]{2,1,0:T(8,128)(2,1)} %pad_maximum_fusion.12), channel_id=1, source_target_pairs={{0,16},{4,20},{8,24},{12,28},{16,0},{20,4},{24,8},{28,12},{1,17},{... | collective-permute-start | bytes 2949128 | tf_op jit(solution)/shard_map/ppermute | solution.py:53
  353.0 48.7 %collective-permute-start.51 = (bf16[256,1024]{1,0:T(8,128)(2,1)S(1)}, bf16[256,1024]{1,0:T(8,128)(2,1)S(1)}, u32[]{:S(2)}, u32[]{:S(2)}) collective-permute-start(bf16[256,1024]{1,0:T(8,128)(2,1)S(1)} %get-tuple-element.234), channel_id=1, source_target_pairs={{0,3},{1,2},{2,1},{3,0},{4,7},{5,6},{6,5},{7,4},{8,11},{9,10},{10,... | collective-permute-start | bytes 1572872 | tf_op jit(solution)/shard_map/ppermute | solution.py:53
  355.0 47.3 %collective-permute-start.50 = (bf16[256,1024]{1,0:T(8,128)(2,1)S(1)}, bf16[256,1024]{1,0:T(8,128)(2,1)S(1)}, u32[]{:S(2)}, u32[]{:S(2)}) collective-permute-start(bf16[256,1024]{1,0:T(8,128)(2,1)S(1)} %get-tuple-element.235), channel_id=1, source_target_pairs={{0,2},{1,3},{2,0},{3,1},{4,6},{5,7},{6,4},{7,5},{8,10},{9,11},{10,... | collective-permute-start | bytes 1572872 | tf_op jit(solution)/shard_map/ppermute | solution.py:53
  357.9 29.3 %collective-permute-start.49 = (bf16[1,64,4096]{2,1,0:T(8,128)(2,1)}, bf16[1,64,4096]{2,1,0:T(8,128)(2,1)S(1)}, u32[]{:S(2)}, u32[]{:S(2)}) collective-permute-start(bf16[1,64,4096]{2,1,0:T(8,128)(2,1)} %get-tuple-element.156), channel_id=1, source_target_pairs={{0,16},{4,20},{8,24},{12,28},{16,0},{20,4},{24,8},{28,12},{1,17},{... | collective-permute-start | bytes 1572872 | tf_op jit(solution)/shard_map/ppermute | solution.py:53
  359.4 28.4 %collective-permute-start.48 = (bf16[1,64,4096]{2,1,0:T(8,128)(2,1)}, bf16[1,64,4096]{2,1,0:T(8,128)(2,1)S(1)}, u32[]{:S(2)}, u32[]{:S(2)}) collective-permute-start(bf16[1,64,4096]{2,1,0:T(8,128)(2,1)} %get-tuple-element.155), channel_id=1, source_target_pairs={{0,8},{4,12},{8,0},{12,4},{16,24},{20,28},{24,16},{28,20},{1,9},{5... | collective-permute-start | bytes 1572872 | tf_op jit(solution)/shard_map/ppermute | solution.py:53
  377.0 24.7 %collective-permute-start.42 = (bf16[256,1024]{1,0:T(8,128)(2,1)S(1)}, bf16[256,1024]{1,0:T(8,128)(2,1)S(1)}, u32[]{:S(2)}, u32[]{:S(2)}) collective-permute-start(bf16[256,1024]{1,0:T(8,128)(2,1)S(1)} %get-tuple-element.233), channel_id=1, source_target_pairs={{0,1},{1,0},{2,3},{3,2},{4,5},{5,4},{6,7},{7,6},{8,9},{9,8},{10,11... | collective-permute-start | bytes 1572872 | tf_op jit(solution)/shard_map/ppermute | solution.py:53
  387.3 12.4 %collective-permute-start.47 = (bf16[1,128,1920]{2,1,0:T(8,128)(2,1)S(1)}, bf16[1,128,1920]{2,1,0:T(8,128)(2,1)S(1)}, u32[]{:S(2)}, u32[]{:S(2)}) collective-permute-start(bf16[1,128,1920]{2,1,0:T(8,128)(2,1)S(1)} %add_convert_fusion.32), channel_id=1, source_target_pairs={{0,8},{4,12},{8,0},{12,4},{16,24},{20,28},{24,16},{28,20},{1,9},{5... | collective-permute-start | bytes 1474568 | tf_op jit(solution)/shard_map/ppermute | solution.py:53
  410.0 13.0 %collective-permute-start.56 = (bf16[32,1920]{1,0:T(8,128)(2,1)}, bf16[32,1920]{1,0:T(8,128)(2,1)S(1)}, u32[]{:S(2)}, u32[]{:S(2)}) collective-permute-start(bf16[32,1920]{1,0:T(8,128)(2,1)} %get-tuple-element.165), channel_id=1, source_target_pairs={{0,2},{1,3},{2,0},{3,1},{4,6},{5,7},{6,4},{7,5},{8,10},{9,11},{10,... | collective-permute-start | bytes 368648 | tf_op jit(solution)/shard_map/ppermute | solution.py:53
  412.0 11.0 %collective-permute-start.55 = (bf16[32,1920]{1,0:T(8,128)(2,1)}, bf16[32,1920]{1,0:T(8,128)(2,1)S(1)}, u32[]{:S(2)}, u32[]{:S(2)}) collective-permute-start(bf16[32,1920]{1,0:T(8,128)(2,1)} %get-tuple-element.164), channel_id=1, source_target_pairs={{0,1},{1,0},{2,3},{3,2},{4,5},{5,4},{6,7},{7,6},{8,9},{9,8},{10,11... | collective-permute-start | bytes 368648 | tf_op jit(solution)/shard_map/ppermute | solution.py:53
  414.3 15.7 %collective-permute-start.52 = (bf16[32,4096]{1,0:T(8,128)(2,1)}, bf16[32,4096]{1,0:T(8,128)(2,1)S(1)}, u32[]{:S(2)}, u32[]{:S(2)}) collective-permute-start(bf16[32,4096]{1,0:T(8,128)(2,1)} %get-tuple-element.159), channel_id=1, source_target_pairs={{0,1},{1,0},{2,3},{3,2},{4,5},{5,4},{6,7},{7,6},{8,9},{9,8},{10,11... | collective-permute-start | bytes 786440 | tf_op jit(solution)/shard_map/ppermute | solution.py:53
  416.3 23.4 %collective-permute-start.53 = (bf16[32,4096]{1,0:T(8,128)(2,1)}, bf16[32,4096]{1,0:T(8,128)(2,1)S(1)}, u32[]{:S(2)}, u32[]{:S(2)}) collective-permute-start(bf16[32,4096]{1,0:T(8,128)(2,1)} %get-tuple-element.160), channel_id=1, source_target_pairs={{0,2},{1,3},{2,0},{3,1},{4,6},{5,7},{6,4},{7,5},{8,10},{9,11},{10,... | collective-permute-start | bytes 786440 | tf_op jit(solution)/shard_map/ppermute | solution.py:53
  417.2 22.5 %collective-permute-start.54 = (bf16[32,4096]{1,0:T(8,128)(2,1)S(1)}, bf16[32,4096]{1,0:T(8,128)(2,1)S(1)}, u32[]{:S(2)}, u32[]{:S(2)}) collective-permute-start(bf16[32,4096]{1,0:T(8,128)(2,1)S(1)} %copy-done.45), channel_id=1, source_target_pairs={{0,3},{1,2},{2,1},{3,0},{4,7},{5,6},{6,5},{7,4},{8,11},{9,10},{10,... | collective-permute-start | bytes 786440 | tf_op jit(solution)/shard_map/ppermute | solution.py:53
  (73 other events, 673.7 us)

commit v2 on v1

--- a/solution.py
+++ b/solution.py
@@ -294,11 +294,11 @@
     columns = []
     for at in range(0, q_ref.shape[1], 128):
         pair = slice(at, at + 128)
-        query, key, value = q_ref[:, pair], k_ref[:, pair], v_ref[:, pair]
+        query, key, value = q_ref[:, pair] * HEAD_DIM ** (-0.5), k_ref[:, pair], v_ref[:, pair]
         outs = []
         for head in range(128 // HEAD_DIM):
             raw = contract(one_head(query, head), key, ((1,), (1,)))
-            raw = raw * HEAD_DIM ** (-0.5) + hidden_keys
+            raw = raw + hidden_keys
             top = jnp.max(raw, axis=-1, keepdims=True)
             expo = jnp.exp(raw - top)
             total = jnp.sum(expo, axis=-1, keepdims=True)
@@ -326,12 +326,12 @@
     scale = HEAD_DIM ** (-0.5)
     for at in range(0, group, 128):
         pair = slice(at, at + 128)
-        query, key, value, grad = q_ref[:, pair], k_ref[:, pair], v_ref[:, pair], grad_ref[:, pair]
+        query, key, value, grad = q_ref[:, pair] * scale, k_ref[:, pair], v_ref[:, pair], grad_ref[:, pair]
         grad_query = grad_key = grad_value = 0.0
         for head in range(128 // HEAD_DIM):
             column = at // HEAD_DIM + head
             own_query, own_grad = one_head(query, head), one_head(grad, head)
-            raw = contract(own_query, key, ((1,), (1,))) * scale + hidden_keys
+            raw = contract(own_query, key, ((1,), (1,))) + hidden_keys
             probs = jnp.exp(raw - lse_ref[:, column : column + 1])
             grad_probs = contract(own_grad, value, ((1,), (1,)))
             inner = jnp.sum(probs * grad_probs, axis=-1, keepdims=True)
@@ -345,7 +345,7 @@
 
     @pl.when(step == pl.num_programs(0) - 1)
     def _():
-        out_ref[:, group : 2 * group] = (sum_ref[:, :group] * scale).astype(out_ref.dtype)
+        out_ref[:, group : 2 * group] = sum_ref[:, :group].astype(out_ref.dtype)
         out_ref[:, 2 * group :] = sum_ref[:, group:].astype(out_ref.dtype)
 
 

time: 449 us -> 448 us (level)
  no operation moved by 1% of the time
where the time goes in v2:
time: 448 us; the launch traced here: 440 us
  waiting for transfers between devices  102 us (23%)
  other arithmetic  92.5 us (21%)
  starting transfers between devices  84.3 us (19%)
  Pallas kernels  63.9 us (14%)
  matrix products  62.4 us (14%)
  local copies, waits for them, and re-layouts  32.3 us (7%)
    ppermute x58, waiting for transfers between devices, swap(): return lax.ppermute(value, axis, [(i, i ^ bit) for i in range(size)])  102 us
    ppermute x58, starting transfers between devices, swap(): return lax.ppermute(value, axis, [(i, i ^ bit) for i in range(size)])  84.3 us
    dot_general x8, matrix products, dot_rows(): jnp.einsum('rk,rn->kn', rows, grad, preferred_element_type=jnp.float32)  22.6 us
    dot_general x8, matrix products, dot(): return jnp.dot(left, right, preferred_element_type=jnp.float32)  22 us
    pallas_call x8, Pallas kernels, pick_columns(): pl.pallas_call(functools.partial(pick_columns_body, table), out_shape=jax...  20.7 us
    pallas_call x1, Pallas kernels, attend_back(): pl.pallas_call(attend_back_body, grid=(length // block,), in_specs=info_s...  19.1 us
    dot_general x8, matrix products, dot_back(): jnp.einsum('rn,kn->rk', grad, weight, preferred_element_type=jnp.float32)  17.8 us
    pallas_call x1, Pallas kernels, attend(): pl.pallas_call(attend_body, grid=(length // block,), in_specs=info_specs...  15.8 us
  transfers between devices with their start and end apart: 58, of which 19 were waited for; matrix products, arithmetic and copies ran while one was open for 32% of the time, Pallas kernels for 12%

profile of v2, /device:TPU:0, one launch (start us, length us, event | category | flops | bytes accessed | tf_op | source)
XLA Modules:
  0.0 440.5 jit_solution(2738778950691050925)
XLA Ops:
  2.5 3.1 collective-permute-start.1
  25.5 3.0 collective-permute-done
  28.5 3.5 collective-permute-start.3
  32.6 9.0 %collective-permute-done.3 = bf16[32,896]{1,0:T(8,128)(2,1)S(1)} collective-permute-done((bf16[32,896]{1,0:T(8,128)(2,1)S(1)}, bf16[32,896]{1,0:T(8,128)(2,1)S(1)}, u32[]{:S(2)}, u32[]{:S(2)}) %collective-permute-start.3) | collective-permute-done | bytes 57376 | tf_op jit(solution)/shard_map/ppermute | solution.py:53
  43.3 3.2 collective-permute-start.5
  50.3 12.0 %collective-permute-done.9 = bf16[64,5120]{1,0:T(8,128)(2,1)S(1)} collective-permute-done((bf16[64,5120]{1,0:T(8,128)(2,1)S(1)}, bf16[64,5120]{1,0:T(8,128)(2,1)S(1)}, u32[]{:S(2)}, u32[]{:S(2)}) %collective-permute-start.9) | collective-permute-done | bytes 655392 | tf_op jit(solution)/shard_map/ppermute | solution.py:53
  65.7 16.3 %collective-permute-done.5 = bf16[256,1024]{1,0:T(8,128)(2,1)S(1)} collective-permute-done((bf16[256,1024]{1,0:T(8,128)(2,1)}, bf16[256,1024]{1,0:T(8,128)(2,1)S(1)}, u32[]{:S(2)}, u32[]{:S(2)}) %collective-permute-start.5) | collective-permute-done | bytes 524320 | tf_op jit(solution)/shard_map/ppermute | solution.py:53
  82.0 9.3 %collective-permute-start.14 = (bf16[128,1024]{1,0:T(8,128)(2,1)}, bf16[128,1024]{1,0:T(8,128)(2,1)}, u32[]{:S(2)}, u32[]{:S(2)}) collective-permute-start(bf16[128,1024]{1,0:T(8,128)(2,1)} %param.34), channel_id=1, source_target_pairs={{0,1},{1,0},{2,3},{3,2},{4,5},{5,4},{6,7},{7,6},{8,9},{9,8},{10,11... | collective-permute-start | bytes 786440 | tf_op jit(solution)/shard_map/ppermute | solution.py:53
  105.1 3.1 fusion.6
  111.8 15.8 %attend.1 = (bf16[1024,256]{1,0:T(8,128)(2,1)}, f32[1024,4]{1,0:T(8,128)}) custom-call(s32[1]{0:T(128)} %copy.132.valid_ref, s32[1024,3]{1,0:T(8,128)} %copy.97.query_ref, s32[3,1024]{1,0:T(4,128)} %pad_add_fusion.key_ref, bf16[1024,768]{1,0:T(8,128)(2,1)} %add_convert_fusion.q_ref.k_ref.v_ref, bf16[1024,768]{1,0:T(8,128)(2,1)} %add_convert_fusion.q_ref.k_ref.v_ref, ...), custom_call_target="tpu_custom_call" | custom-call | flops 4294967296 | bytes 8388608 | tf_op jit(solution)/shard_map/attend/pallas_call | solution.py:366
  127.7 2.7 collective-permute-done.18.refs_3_
  130.4 4.6 %place_rows.2 = bf16[512,5120]{1,0:T(8,128)(2,1)} custom-call(bf16[128,5120]{1,0:T(8,128)(2,1)} %copy-done.19, bf16[128,5120]{1,0:T(8,128)(2,1)} %pad_maximum_fusion.3.refs_1_, bf16[128,5120]{1,0:T(8,128)(2,1)} %collective-permute-done.17.refs_2_, bf16[128,5120]{1,0:T(8,128)(2,1)} %collective-permute-done.18.refs_3_), custom_call_target="tpu_custom_call" | custom-call | bytes 10485760 | tf_op jit(solution)/shard_map/place_rows/pallas_call | solution.py:142
  141.5 3.6 collective-permute-done.21
  145.1 4.8 %collective-permute-start.19 = (bf16[256,256]{1,0:T(8,128)(2,1)S(1)}, bf16[256,256]{1,0:T(8,128)(2,1)S(1)}, u32[]{:S(2)}, u32[]{:S(2)}) collective-permute-start(bf16[256,256]{1,0:T(8,128)(2,1)S(1)} %get-tuple-element.269), channel_id=1, source_target_pairs={{0,1},{1,0},{2,3},{3,2},{4,5},{5,4},{6,7},{7,6},{8,9},{9,8},{10,11... | collective-permute-start | bytes 393224 | tf_op jit(solution)/shard_map/ppermute | solution.py:53
  151.8 2.7 collective-permute-done.19
  163.8 3.1 convert_add_fusion.1
  173.5 3.6 fusion.26
  177.2 5.5 %fusion.in_ref = f32[256,4096]{1,0:T(8,128)} fusion(f32[256,4096]{1,0:T(8,128)S(1)} %fusion.26, bf16[512,5120]{1,0:T(8,128)(2,1)} %collective-permute-done.24, f32[4096]{0:T(1024)S(1)} %bitcast.185, bf16[256,1024]{1,0:T(8,128)(2,1)S(1)} %add_convert_fusion.30), kind=kOutput, calls=%fused_computation.6 | convolution fusion | flops 1075838976 | bytes 12861440 | tf_op jit(solution)/shard_map/dot_general | solution.py:248
  182.6 4.5 %pick_columns.11 = f32[256,4096]{1,0:T(8,128)} custom-call(s32[1]{0:T(128)} %bitcast.6.flip_ref, f32[256,4096]{1,0:T(8,128)} %fusion.in_ref), custom_call_target="tpu_custom_call" | custom-call | tf_op jit(solution)/shard_map/pick_columns/pallas_call | solution.py:97
  187.2 3.5 fusion.13
  190.6 3.4 convolution_convert_fusion.3
  194.0 3.6 place_rows.3
  204.4 2.6 add_convert_fusion.27
  209.3 3.9 fusion.124
  213.2 3.7 fusion.20.in_ref
  216.9 3.2 pick_columns.12
  220.0 5.2 %convolution_convert_fusion.1 = bf16[512,4096]{1,0:T(8,128)(2,1)} fusion(bf16[256,4096]{1,0:T(8,128)(2,1)} %pick_columns.12, bf16[256,1024]{1,0:T(8,128)(2,1)} %copy-done.20), kind=kOutput, calls=%fused_computation.4 | convolution fusion | flops 1075838976 | bytes 6553600 | tf_op jit(solution)/shard_map/rk,rn->kn/dot_general | solution.py:256
  225.2 3.5 fusion.24
  228.7 3.6 fusion.21
  247.4 2.8 collective-permute-start.31
  253.2 2.6 convolution_convert_fusion.5
  255.8 4.2 convolution_convert_fusion
  260.0 3.6 fusion.47
  272.9 4.2 fusion.110
  280.1 2.6 collective-permute-done.29
  284.4 3.8 add_convert_fusion.22
  296.9 19.1 %attend_back.1 = bf16[1024,768]{1,0:T(8,128)(2,1)} custom-call(s32[1]{0:T(128)} %copy.132.valid_ref, s32[1024,3]{1,0:T(8,128)} %copy.97.query_ref, s32[3,1024]{1,0:T(4,128)} %pad_add_fusion.key_ref, f32[1024,4]{1,0:T(8,128)} %get-tuple-element.137.lse_ref, bf16[1024,768]{1,0:T(8,128)(2,1)} %add_convert_fusion.q_ref.k_ref.v_ref, ...), custom_call_target="tpu_custom_call" | custom-call | flops 10737418240 | bytes 16777216 | tf_op jit(solution)/shard_map/attend_back/pallas_call | solution.py:390
  316.0 3.0 fusion.68
  333.2 2.5 fusion.29
  335.7 3.5 convolution_convert_fusion.7
  339.3 3.4 add_convert_fusion.8
  354.6 2.9 collective-permute-start.50
  361.7 14.9 %collective-permute-done.46 = bf16[2,128,1920]{2,1,0:T(8,128)(2,1)} collective-permute-done((bf16[2,128,1920]{2,1,0:T(8,128)(2,1)}, bf16[2,128,1920]{2,1,0:T(8,128)(2,1)}, u32[]{:S(2)}, u32[]{:S(2)}) %collective-permute-start.46) | collective-permute-done | bytes 983072 | tf_op jit(solution)/shard_map/ppermute | solution.py:53
  376.6 3.4 collective-permute-start.42
  381.2 5.7 %collective-permute-done.49 = bf16[1,64,4096]{2,1,0:T(8,128)(2,1)S(1)} collective-permute-done((bf16[1,64,4096]{2,1,0:T(8,128)(2,1)}, bf16[1,64,4096]{2,1,0:T(8,128)(2,1)S(1)}, u32[]{:S(2)}, u32[]{:S(2)}) %collective-permute-start.49) | collective-permute-done | bytes 524320 | tf_op jit(solution)/shard_map/ppermute | solution.py:53
  391.4 7.9 %collective-permute-done.47 = bf16[1,128,1920]{2,1,0:T(8,128)(2,1)S(1)} collective-permute-done((bf16[1,128,1920]{2,1,0:T(8,128)(2,1)S(1)}, bf16[1,128,1920]{2,1,0:T(8,128)(2,1)S(1)}, u32[]{:S(2)}, u32[]{:S(2)}) %collective-permute-start.47) | collective-permute-done | bytes 491552 | tf_op jit(solution)/shard_map/ppermute | solution.py:53
  418.4 4.1 collective-permute-done.56
  429.6 9.8 %collective-permute-done.53 = bf16[32,4096]{1,0:T(8,128)(2,1)S(1)} collective-permute-done((bf16[32,4096]{1,0:T(8,128)(2,1)}, bf16[32,4096]{1,0:T(8,128)(2,1)S(1)}, u32[]{:S(2)}, u32[]{:S(2)}) %collective-permute-start.53) | collective-permute-done | bytes 262176 | tf_op jit(solution)/shard_map/ppermute | solution.py:53
  (414 shorter events, 183.1 us)
Async XLA Ops:
  2.5 30.1 %collective-permute-start.1 = (bf16[32,5120]{1,0:T(8,128)(2,1)S(1)}, bf16[32,5120]{1,0:T(8,128)(2,1)S(1)}, u32[]{:S(2)}, u32[]{:S(2)}) collective-permute-start(bf16[32,5120]{1,0:T(8,128)(2,1)S(1)} %constant_dynamic-update-slice_fusion), channel_id=1, source_target_pairs={{0,1},{1,0},{2,3},{3,2},{4,5},{5,4},{6,7},{7,6},{8,9},{9,8},{10,11... | collective-permute-start | bytes 983048 | tf_op jit(solution)/shard_map/ppermute | solution.py:53
  5.6 27.0 %collective-permute-start.7 = (bf16[32,5120]{1,0:T(8,128)(2,1)S(1)}, bf16[32,5120]{1,0:T(8,128)(2,1)S(1)}, u32[]{:S(2)}, u32[]{:S(2)}) collective-permute-start(bf16[32,5120]{1,0:T(8,128)(2,1)S(1)} %constant_dynamic-update-slice_fusion), channel_id=1, source_target_pairs={{0,3},{1,2},{2,1},{3,0},{4,7},{5,6},{6,5},{7,4},{8,11},{9,10},{10,... | collective-permute-start | bytes 983048 | tf_op jit(solution)/shard_map/ppermute | solution.py:53
  8.1 33.5 %collective-permute-start.4 = (bf16[32,5120]{1,0:T(8,128)(2,1)S(1)}, bf16[32,5120]{1,0:T(8,128)(2,1)S(1)}, u32[]{:S(2)}, u32[]{:S(2)}) collective-permute-start(bf16[32,5120]{1,0:T(8,128)(2,1)S(1)} %constant_dynamic-update-slice_fusion), channel_id=1, source_target_pairs={{0,2},{1,3},{2,0},{3,1},{4,6},{5,7},{6,4},{7,5},{8,10},{9,11},{10,... | collective-permute-start | bytes 983048 | tf_op jit(solution)/shard_map/ppermute | solution.py:53
  14.0 14.5 %collective-permute-start = (bf16[32,896]{1,0:T(8,128)(2,1)S(1)}, bf16[32,896]{1,0:T(8,128)(2,1)S(1)}, u32[]{:S(2)}, u32[]{:S(2)}) collective-permute-start(bf16[32,896]{1,0:T(8,128)(2,1)S(1)} %get-tuple-element.301), channel_id=1, source_target_pairs={{0,1},{1,0},{2,3},{3,2},{4,5},{5,4},{6,7},{7,6},{8,9},{9,8},{10,11... | collective-permute-start | bytes 172040 | tf_op jit(solution)/shard_map/ppermute | solution.py:53
  15.9 16.7 %collective-permute-start.6 = (bf16[32,896]{1,0:T(8,128)(2,1)S(1)}, bf16[32,896]{1,0:T(8,128)(2,1)S(1)}, u32[]{:S(2)}, u32[]{:S(2)}) collective-permute-start(bf16[32,896]{1,0:T(8,128)(2,1)S(1)} %get-tuple-element.300), channel_id=1, source_target_pairs={{0,3},{1,2},{2,1},{3,0},{4,7},{5,6},{6,5},{7,4},{8,11},{9,10},{10,... | collective-permute-start | bytes 172040 | tf_op jit(solution)/shard_map/ppermute | solution.py:53
  28.5 13.1 %collective-permute-start.3 = (bf16[32,896]{1,0:T(8,128)(2,1)S(1)}, bf16[32,896]{1,0:T(8,128)(2,1)S(1)}, u32[]{:S(2)}, u32[]{:S(2)}) collective-permute-start(bf16[32,896]{1,0:T(8,128)(2,1)S(1)} %get-tuple-element.302), channel_id=1, source_target_pairs={{0,2},{1,3},{2,0},{3,1},{4,6},{5,7},{6,4},{7,5},{8,10},{9,11},{10,... | collective-permute-start | bytes 172040 | tf_op jit(solution)/shard_map/ppermute | solution.py:53
  43.3 22.4 %collective-permute-start.2 = (bf16[256,1024]{1,0:T(8,128)(2,1)}, bf16[256,1024]{1,0:T(8,128)(2,1)S(1)}, u32[]{:S(2)}, u32[]{:S(2)}) collective-permute-start(bf16[256,1024]{1,0:T(8,128)(2,1)} %pick_columns.8), channel_id=1, source_target_pairs={{0,1},{1,0},{2,3},{3,2},{4,5},{5,4},{6,7},{7,6},{8,9},{9,8},{10,11... | collective-permute-start | bytes 1572872 | tf_op jit(solution)/shard_map/ppermute | solution.py:53
  43.3 38.7 %collective-permute-start.5 = (bf16[256,1024]{1,0:T(8,128)(2,1)}, bf16[256,1024]{1,0:T(8,128)(2,1)S(1)}, u32[]{:S(2)}, u32[]{:S(2)}) collective-permute-start(bf16[256,1024]{1,0:T(8,128)(2,1)} %pick_columns.8), channel_id=1, source_target_pairs={{0,2},{1,3},{2,0},{3,1},{4,6},{5,7},{6,4},{7,5},{8,10},{9,11},{10,... | collective-permute-start | bytes 1572872 | tf_op jit(solution)/shard_map/ppermute | solution.py:53
  46.6 35.5 %collective-permute-start.8 = (bf16[256,1024]{1,0:T(8,128)(2,1)}, bf16[256,1024]{1,0:T(8,128)(2,1)S(1)}, u32[]{:S(2)}, u32[]{:S(2)}) collective-permute-start(bf16[256,1024]{1,0:T(8,128)(2,1)} %pick_columns.8), channel_id=1, source_target_pairs={{0,3},{1,2},{2,1},{3,0},{4,7},{5,6},{6,5},{7,4},{8,11},{9,10},{10,... | collective-permute-start | bytes 1572872 | tf_op jit(solution)/shard_map/ppermute | solution.py:53
  47.9 14.4 %collective-permute-start.9 = (bf16[64,5120]{1,0:T(8,128)(2,1)S(1)}, bf16[64,5120]{1,0:T(8,128)(2,1)S(1)}, u32[]{:S(2)}, u32[]{:S(2)}) collective-permute-start(bf16[64,5120]{1,0:T(8,128)(2,1)S(1)} %pad_maximum_fusion.13), channel_id=1, source_target_pairs={{0,8},{4,12},{8,0},{12,4},{16,24},{20,28},{24,16},{28,20},{1,9},{5... | collective-permute-start | bytes 1966088 | tf_op jit(solution)/shard_map/ppermute | solution.py:53
  48.6 15.3 %collective-permute-start.10 = (bf16[64,5120]{1,0:T(8,128)(2,1)S(1)}, bf16[64,5120]{1,0:T(8,128)(2,1)S(1)}, u32[]{:S(2)}, u32[]{:S(2)}) collective-permute-start(bf16[64,5120]{1,0:T(8,128)(2,1)S(1)} %pad_maximum_fusion.14), channel_id=1, source_target_pairs={{0,16},{4,20},{8,24},{12,28},{16,0},{20,4},{24,8},{28,12},{1,17},{... | collective-permute-start | bytes 1966088 | tf_op jit(solution)/shard_map/ppermute | solution.py:53
  62.3 33.0 %collective-permute-start.12 = (bf16[256,896]{1,0:T(8,128)(2,1)S(1)}, bf16[256,896]{1,0:T(8,128)(2,1)S(1)}, u32[]{:S(2)}, u32[]{:S(2)}) collective-permute-start(bf16[256,896]{1,0:T(8,128)(2,1)S(1)} %get-tuple-element.274), channel_id=1, source_target_pairs={{0,16},{4,20},{8,24},{12,28},{16,0},{20,4},{24,8},{28,12},{1,17},{... | collective-permute-start | bytes 1376264 | tf_op jit(solution)/shard_map/ppermute | solution.py:53
  82.0 45.6 %collective-permute-start.14 = (bf16[128,1024]{1,0:T(8,128)(2,1)}, bf16[128,1024]{1,0:T(8,128)(2,1)}, u32[]{:S(2)}, u32[]{:S(2)}) collective-permute-start(bf16[128,1024]{1,0:T(8,128)(2,1)} %param.34), channel_id=1, source_target_pairs={{0,1},{1,0},{2,3},{3,2},{4,5},{5,4},{6,7},{7,6},{8,9},{9,8},{10,11... | collective-permute-start | bytes 786440 | tf_op jit(solution)/shard_map/ppermute | solution.py:53
  91.3 36.3 %collective-permute-start.15 = (bf16[128,1024]{1,0:T(8,128)(2,1)}, bf16[128,1024]{1,0:T(8,128)(2,1)}, u32[]{:S(2)}, u32[]{:S(2)}) collective-permute-start(bf16[128,1024]{1,0:T(8,128)(2,1)} %param.34), channel_id=1, source_target_pairs={{0,2},{1,3},{2,0},{3,1},{4,6},{5,7},{6,4},{7,5},{8,10},{9,11},{10,... | collective-permute-start | bytes 786440 | tf_op jit(solution)/shard_map/ppermute | solution.py:53
  92.2 35.5 %collective-permute-start.16 = (bf16[128,1024]{1,0:T(8,128)(2,1)}, bf16[128,1024]{1,0:T(8,128)(2,1)}, u32[]{:S(2)}, u32[]{:S(2)}) collective-permute-start(bf16[128,1024]{1,0:T(8,128)(2,1)} %param.34), channel_id=1, source_target_pairs={{0,3},{1,2},{2,1},{3,0},{4,7},{5,6},{6,5},{7,4},{8,11},{9,10},{10,... | collective-permute-start | bytes 786440 | tf_op jit(solution)/shard_map/ppermute | solution.py:53
  93.7 34.0 %collective-permute-start.17 = (bf16[128,5120]{1,0:T(8,128)(2,1)S(1)}, bf16[128,5120]{1,0:T(8,128)(2,1)}, u32[]{:S(2)}, u32[]{:S(2)}) collective-permute-start(bf16[128,5120]{1,0:T(8,128)(2,1)S(1)} %pad_maximum_fusion.2.refs_0_), channel_id=1, source_target_pairs={{0,16},{4,20},{8,24},{12,28},{16,0},{20,4},{24,8},{28,12},{1,17},{... | collective-permute-start | bytes 3932168 | tf_op jit(solution)/shard_map/ppermute | solution.py:53
  98.9 31.6 %collective-permute-start.18 = (bf16[128,5120]{1,0:T(8,128)(2,1)}, bf16[128,5120]{1,0:T(8,128)(2,1)}, u32[]{:S(2)}, u32[]{:S(2)}) collective-permute-start(bf16[128,5120]{1,0:T(8,128)(2,1)} %pad_maximum_fusion.3.refs_1_), channel_id=1, source_target_pairs={{0,8},{4,12},{8,0},{12,4},{16,24},{20,28},{24,16},{28,20},{1,9},{5... | collective-permute-start | bytes 3932168 | tf_op jit(solution)/shard_map/ppermute | solution.py:53
  136.6 27.2 %collective-permute-start.24 = (bf16[512,5120]{1,0:T(8,128)(2,1)}, bf16[512,5120]{1,0:T(8,128)(2,1)}, u32[]{:S(2)}, u32[]{:S(2)}) collective-permute-start(bf16[512,5120]{1,0:T(8,128)(2,1)} %place_rows.2), channel_id=1, source_target_pairs={{0,4},{4,0},{8,12},{12,8},{16,20},{20,16},{24,28},{28,24},{1,5},{5... | collective-permute-start | bytes 15728648 | tf_op jit(solution)/shard_map/ppermute | solution.py:53
  139.2 16.1 %collective-permute-start.22 = (bf16[256,1024]{1,0:T(8,128)(2,1)S(1)}, bf16[256,1024]{1,0:T(8,128)(2,1)}, u32[]{:S(2)}, u32[]{:S(2)}) collective-permute-start(bf16[256,1024]{1,0:T(8,128)(2,1)S(1)} %get-tuple-element.253), channel_id=1, source_target_pairs={{0,8},{4,12},{8,0},{12,4},{16,24},{20,28},{24,16},{28,20},{1,9},{5... | collective-permute-start | bytes 1572872 | tf_op jit(solution)/shard_map/ppermute | solution.py:53
  139.8 17.6 %collective-permute-start.23 = (bf16[256,1024]{1,0:T(8,128)(2,1)S(1)}, bf16[256,1024]{1,0:T(8,128)(2,1)}, u32[]{:S(2)}, u32[]{:S(2)}) collective-permute-start(bf16[256,1024]{1,0:T(8,128)(2,1)S(1)} %get-tuple-element.252), channel_id=1, source_target_pairs={{0,16},{4,20},{8,24},{12,28},{16,0},{20,4},{24,8},{28,12},{1,17},{... | collective-permute-start | bytes 1572872 | tf_op jit(solution)/shard_map/ppermute | solution.py:53
  141.2 10.5 %collective-permute-start.20 = (bf16[256,256]{1,0:T(8,128)(2,1)S(1)}, bf16[256,256]{1,0:T(8,128)(2,1)S(1)}, u32[]{:S(2)}, u32[]{:S(2)}) collective-permute-start(bf16[256,256]{1,0:T(8,128)(2,1)S(1)} %get-tuple-element.268), channel_id=1, source_target_pairs={{0,2},{1,3},{2,0},{3,1},{4,6},{5,7},{6,4},{7,5},{8,10},{9,11},{10,... | collective-permute-start | bytes 393224 | tf_op jit(solution)/shard_map/ppermute | solution.py:53
  159.5 27.6 %collective-permute-start.25 = (bf16[512,1024]{1,0:T(8,128)(2,1)}, bf16[512,1024]{1,0:T(8,128)(2,1)}, u32[]{:S(2)}, u32[]{:S(2)}) collective-permute-start(bf16[512,1024]{1,0:T(8,128)(2,1)} %pad_maximum_fusion.5.refs_0_), channel_id=1, source_target_pairs={{0,16},{4,20},{8,24},{12,28},{16,0},{20,4},{24,8},{28,12},{1,17},{... | collective-permute-start | bytes 3145736 | tf_op jit(solution)/shard_map/ppermute | solution.py:53
  160.0 27.1 %collective-permute-start.26 = (bf16[512,1024]{1,0:T(8,128)(2,1)}, bf16[512,1024]{1,0:T(8,128)(2,1)}, u32[]{:S(2)}, u32[]{:S(2)}) collective-permute-start(bf16[512,1024]{1,0:T(8,128)(2,1)} %pad_maximum_fusion.6.refs_1_), channel_id=1, source_target_pairs={{0,8},{4,12},{8,0},{12,4},{16,24},{20,28},{24,16},{28,20},{1,9},{5... | collective-permute-start | bytes 3145736 | tf_op jit(solution)/shard_map/ppermute | solution.py:53
  197.6 11.7 %collective-permute-start.27 = (bf16[2048,1024]{1,0:T(8,128)(2,1)}, bf16[2048,1024]{1,0:T(8,128)(2,1)}, u32[]{:S(2)}, u32[]{:S(2)}) collective-permute-start(bf16[2048,1024]{1,0:T(8,128)(2,1)} %place_rows.3), channel_id=1, source_target_pairs={{0,4},{4,0},{8,12},{12,8},{16,20},{20,16},{24,28},{28,24},{1,5},{5... | collective-permute-start | bytes 12582920 | tf_op jit(solution)/shard_map/ppermute | solution.py:53
  233.4 54.9 %collective-permute-start.34 = (bf16[512,4096]{1,0:T(8,128)(2,1)}, bf16[512,4096]{1,0:T(8,128)(2,1)}, u32[]{:S(2)}, u32[]{:S(2)}) collective-permute-start(bf16[512,4096]{1,0:T(8,128)(2,1)} %convolution_convert_fusion.1), channel_id=1, source_target_pairs={{0,4},{4,0},{8,12},{12,8},{16,20},{20,16},{24,28},{28,24},{1,5},{5... | collective-permute-start | bytes 12582920 | tf_op jit(solution)/shard_map/ppermute | solution.py:53
  247.4 30.3 %collective-permute-start.31 = (bf16[256,256]{1,0:T(8,128)(2,1)}, bf16[256,256]{1,0:T(8,128)(2,1)S(1)}, u32[]{:S(2)}, u32[]{:S(2)}) collective-permute-start(bf16[256,256]{1,0:T(8,128)(2,1)} %get-tuple-element.263), channel_id=1, source_target_pairs={{0,3},{1,2},{2,1},{3,0},{4,7},{5,6},{6,5},{7,4},{8,11},{9,10},{10,... | collective-permute-start | bytes 393224 | tf_op jit(solution)/shard_map/ppermute | solution.py:53
  250.2 34.2 %collective-permute-start.33 = (bf16[2,256,1024]{2,1,0:T(8,128)(2,1)}, bf16[2,256,1024]{2,1,0:T(8,128)(2,1)}, u32[]{:S(2)}, u32[]{:S(2)}) collective-permute-start(bf16[2,256,1024]{2,1,0:T(8,128)(2,1)} %pad_maximum_fusion.8), channel_id=1, source_target_pairs={{0,8},{4,12},{8,0},{12,4},{16,24},{20,28},{24,16},{28,20},{1,9},{5... | collective-permute-start | bytes 3145736 | tf_op jit(solution)/shard_map/ppermute | solution.py:53
  251.7 32.8 %collective-permute-start.32 = (bf16[2,256,1024]{2,1,0:T(8,128)(2,1)}, bf16[2,256,1024]{2,1,0:T(8,128)(2,1)}, u32[]{:S(2)}, u32[]{:S(2)}) collective-permute-start(bf16[2,256,1024]{2,1,0:T(8,128)(2,1)} %pad_maximum_fusion.7), channel_id=1, source_target_pairs={{0,16},{4,20},{8,24},{12,28},{16,0},{20,4},{24,8},{28,12},{1,17},{... | collective-permute-start | bytes 3145736 | tf_op jit(solution)/shard_map/ppermute | solution.py:53
  268.9 11.2 %collective-permute-start.30 = (bf16[256,256]{1,0:T(8,128)(2,1)}, bf16[256,256]{1,0:T(8,128)(2,1)}, u32[]{:S(2)}, u32[]{:S(2)}) collective-permute-start(bf16[256,256]{1,0:T(8,128)(2,1)} %get-tuple-element.264), channel_id=1, source_target_pairs={{0,2},{1,3},{2,0},{3,1},{4,6},{5,7},{6,4},{7,5},{8,10},{9,11},{10,... | collective-permute-start | bytes 393224 | tf_op jit(solution)/shard_map/ppermute | solution.py:53
  292.8 23.2 %collective-permute-start.36 = (bf16[1,256,1024]{2,1,0:T(8,128)(2,1)}, bf16[1,256,1024]{2,1,0:T(8,128)(2,1)S(1)}, u32[]{:S(2)}, u32[]{:S(2)}) collective-permute-start(bf16[1,256,1024]{2,1,0:T(8,128)(2,1)} %get-tuple-element.144), channel_id=1, source_target_pairs={{0,16},{4,20},{8,24},{12,28},{16,0},{20,4},{24,8},{28,12},{1,17},{... | collective-permute-start | bytes 1572872 | tf_op jit(solution)/shard_map/ppermute | solution.py:53
  293.3 22.7 %collective-permute-start.35 = (bf16[1,256,1024]{2,1,0:T(8,128)(2,1)}, bf16[1,256,1024]{2,1,0:T(8,128)(2,1)}, u32[]{:S(2)}, u32[]{:S(2)}) collective-permute-start(bf16[1,256,1024]{2,1,0:T(8,128)(2,1)} %get-tuple-element.143), channel_id=1, source_target_pairs={{0,8},{4,12},{8,0},{12,4},{16,24},{20,28},{24,16},{28,20},{1,9},{5... | collective-permute-start | bytes 1572872 | tf_op jit(solution)/shard_map/ppermute | solution.py:53
  293.8 45.5 %collective-permute-start.38 = (bf16[2,64,4096]{2,1,0:T(8,128)(2,1)}, bf16[2,64,4096]{2,1,0:T(8,128)(2,1)}, u32[]{:S(2)}, u32[]{:S(2)}) collective-permute-start(bf16[2,64,4096]{2,1,0:T(8,128)(2,1)} %pad_maximum_fusion.11), channel_id=1, source_target_pairs={{0,8},{4,12},{8,0},{12,4},{16,24},{20,28},{24,16},{28,20},{1,9},{5... | collective-permute-start | bytes 3145736 | tf_op jit(solution)/shard_map/ppermute | solution.py:53
  295.3 43.9 %collective-permute-start.37 = (bf16[2,64,4096]{2,1,0:T(8,128)(2,1)}, bf16[2,64,4096]{2,1,0:T(8,128)(2,1)}, u32[]{:S(2)}, u32[]{:S(2)}) collective-permute-start(bf16[2,64,4096]{2,1,0:T(8,128)(2,1)} %pad_maximum_fusion.10), channel_id=1, source_target_pairs={{0,16},{4,20},{8,24},{12,28},{16,0},{20,4},{24,8},{28,12},{1,17},{... | collective-permute-start | bytes 3145736 | tf_op jit(solution)/shard_map/ppermute | solution.py:53
  322.1 20.6 %collective-permute-start.39 = (bf16[128,1024]{1,0:T(8,128)(2,1)}, bf16[128,1024]{1,0:T(8,128)(2,1)}, u32[]{:S(2)}, u32[]{:S(2)}) collective-permute-start(bf16[128,1024]{1,0:T(8,128)(2,1)} %get-tuple-element.149), channel_id=1, source_target_pairs={{0,1},{1,0},{2,3},{3,2},{4,5},{5,4},{6,7},{7,6},{8,9},{9,8},{10,11... | collective-permute-start | bytes 786440 | tf_op jit(solution)/shard_map/ppermute | solution.py:53
  324.1 20.3 %collective-permute-start.40 = (bf16[128,1024]{1,0:T(8,128)(2,1)}, bf16[128,1024]{1,0:T(8,128)(2,1)}, u32[]{:S(2)}, u32[]{:S(2)}) collective-permute-start(bf16[128,1024]{1,0:T(8,128)(2,1)} %get-tuple-element.150), channel_id=1, source_target_pairs={{0,2},{1,3},{2,0},{3,1},{4,6},{5,7},{6,4},{7,5},{8,10},{9,11},{10,... | collective-permute-start | bytes 786440 | tf_op jit(solution)/shard_map/ppermute | solution.py:53
  325.1 19.3 %collective-permute-start.41 = (bf16[128,1024]{1,0:T(8,128)(2,1)}, bf16[128,1024]{1,0:T(8,128)(2,1)}, u32[]{:S(2)}, u32[]{:S(2)}) collective-permute-start(bf16[128,1024]{1,0:T(8,128)(2,1)} %get-tuple-element.151), channel_id=1, source_target_pairs={{0,3},{1,2},{2,1},{3,0},{4,7},{5,6},{6,5},{7,4},{8,11},{9,10},{10,... | collective-permute-start | bytes 786440 | tf_op jit(solution)/shard_map/ppermute | solution.py:53
  351.6 24.9 %collective-permute-start.46 = (bf16[2,128,1920]{2,1,0:T(8,128)(2,1)}, bf16[2,128,1920]{2,1,0:T(8,128)(2,1)}, u32[]{:S(2)}, u32[]{:S(2)}) collective-permute-start(bf16[2,128,1920]{2,1,0:T(8,128)(2,1)} %pad_maximum_fusion.12), channel_id=1, source_target_pairs={{0,16},{4,20},{8,24},{12,28},{16,0},{20,4},{24,8},{28,12},{1,17},{... | collective-permute-start | bytes 2949128 | tf_op jit(solution)/shard_map/ppermute | solution.py:53
  352.6 48.7 %collective-permute-start.51 = (bf16[256,1024]{1,0:T(8,128)(2,1)S(1)}, bf16[256,1024]{1,0:T(8,128)(2,1)S(1)}, u32[]{:S(2)}, u32[]{:S(2)}) collective-permute-start(bf16[256,1024]{1,0:T(8,128)(2,1)S(1)} %get-tuple-element.234), channel_id=1, source_target_pairs={{0,3},{1,2},{2,1},{3,0},{4,7},{5,6},{6,5},{7,4},{8,11},{9,10},{10,... | collective-permute-start | bytes 1572872 | tf_op jit(solution)/shard_map/ppermute | solution.py:53
  354.6 47.3 %collective-permute-start.50 = (bf16[256,1024]{1,0:T(8,128)(2,1)S(1)}, bf16[256,1024]{1,0:T(8,128)(2,1)S(1)}, u32[]{:S(2)}, u32[]{:S(2)}) collective-permute-start(bf16[256,1024]{1,0:T(8,128)(2,1)S(1)} %get-tuple-element.235), channel_id=1, source_target_pairs={{0,2},{1,3},{2,0},{3,1},{4,6},{5,7},{6,4},{7,5},{8,10},{9,11},{10,... | collective-permute-start | bytes 1572872 | tf_op jit(solution)/shard_map/ppermute | solution.py:53
  357.5 29.3 %collective-permute-start.49 = (bf16[1,64,4096]{2,1,0:T(8,128)(2,1)}, bf16[1,64,4096]{2,1,0:T(8,128)(2,1)S(1)}, u32[]{:S(2)}, u32[]{:S(2)}) collective-permute-start(bf16[1,64,4096]{2,1,0:T(8,128)(2,1)} %get-tuple-element.156), channel_id=1, source_target_pairs={{0,16},{4,20},{8,24},{12,28},{16,0},{20,4},{24,8},{28,12},{1,17},{... | collective-permute-start | bytes 1572872 | tf_op jit(solution)/shard_map/ppermute | solution.py:53
  359.1 28.4 %collective-permute-start.48 = (bf16[1,64,4096]{2,1,0:T(8,128)(2,1)}, bf16[1,64,4096]{2,1,0:T(8,128)(2,1)S(1)}, u32[]{:S(2)}, u32[]{:S(2)}) collective-permute-start(bf16[1,64,4096]{2,1,0:T(8,128)(2,1)} %get-tuple-element.155), channel_id=1, source_target_pairs={{0,8},{4,12},{8,0},{12,4},{16,24},{20,28},{24,16},{28,20},{1,9},{5... | collective-permute-start | bytes 1572872 | tf_op jit(solution)/shard_map/ppermute | solution.py:53
  376.6 24.7 %collective-permute-start.42 = (bf16[256,1024]{1,0:T(8,128)(2,1)S(1)}, bf16[256,1024]{1,0:T(8,128)(2,1)S(1)}, u32[]{:S(2)}, u32[]{:S(2)}) collective-permute-start(bf16[256,1024]{1,0:T(8,128)(2,1)S(1)} %get-tuple-element.233), channel_id=1, source_target_pairs={{0,1},{1,0},{2,3},{3,2},{4,5},{5,4},{6,7},{7,6},{8,9},{9,8},{10,11... | collective-permute-start | bytes 1572872 | tf_op jit(solution)/shard_map/ppermute | solution.py:53
  386.9 12.4 %collective-permute-start.47 = (bf16[1,128,1920]{2,1,0:T(8,128)(2,1)S(1)}, bf16[1,128,1920]{2,1,0:T(8,128)(2,1)S(1)}, u32[]{:S(2)}, u32[]{:S(2)}) collective-permute-start(bf16[1,128,1920]{2,1,0:T(8,128)(2,1)S(1)} %add_convert_fusion.32), channel_id=1, source_target_pairs={{0,8},{4,12},{8,0},{12,4},{16,24},{20,28},{24,16},{28,20},{1,9},{5... | collective-permute-start | bytes 1474568 | tf_op jit(solution)/shard_map/ppermute | solution.py:53
  409.6 13.0 %collective-permute-start.56 = (bf16[32,1920]{1,0:T(8,128)(2,1)}, bf16[32,1920]{1,0:T(8,128)(2,1)S(1)}, u32[]{:S(2)}, u32[]{:S(2)}) collective-permute-start(bf16[32,1920]{1,0:T(8,128)(2,1)} %get-tuple-element.165), channel_id=1, source_target_pairs={{0,2},{1,3},{2,0},{3,1},{4,6},{5,7},{6,4},{7,5},{8,10},{9,11},{10,... | collective-permute-start | bytes 368648 | tf_op jit(solution)/shard_map/ppermute | solution.py:53
  411.6 10.9 %collective-permute-start.55 = (bf16[32,1920]{1,0:T(8,128)(2,1)}, bf16[32,1920]{1,0:T(8,128)(2,1)S(1)}, u32[]{:S(2)}, u32[]{:S(2)}) collective-permute-start(bf16[32,1920]{1,0:T(8,128)(2,1)} %get-tuple-element.164), channel_id=1, source_target_pairs={{0,1},{1,0},{2,3},{3,2},{4,5},{5,4},{6,7},{7,6},{8,9},{9,8},{10,11... | collective-permute-start | bytes 368648 | tf_op jit(solution)/shard_map/ppermute | solution.py:53
  413.9 15.6 %collective-permute-start.52 = (bf16[32,4096]{1,0:T(8,128)(2,1)}, bf16[32,4096]{1,0:T(8,128)(2,1)S(1)}, u32[]{:S(2)}, u32[]{:S(2)}) collective-permute-start(bf16[32,4096]{1,0:T(8,128)(2,1)} %get-tuple-element.159), channel_id=1, source_target_pairs={{0,1},{1,0},{2,3},{3,2},{4,5},{5,4},{6,7},{7,6},{8,9},{9,8},{10,11... | collective-permute-start | bytes 786440 | tf_op jit(solution)/shard_map/ppermute | solution.py:53
  415.9 23.4 %collective-permute-start.53 = (bf16[32,4096]{1,0:T(8,128)(2,1)}, bf16[32,4096]{1,0:T(8,128)(2,1)S(1)}, u32[]{:S(2)}, u32[]{:S(2)}) collective-permute-start(bf16[32,4096]{1,0:T(8,128)(2,1)} %get-tuple-element.160), channel_id=1, source_target_pairs={{0,2},{1,3},{2,0},{3,1},{4,6},{5,7},{6,4},{7,5},{8,10},{9,11},{10,... | collective-permute-start | bytes 786440 | tf_op jit(solution)/shard_map/ppermute | solution.py:53
  416.8 22.5 %collective-permute-start.54 = (bf16[32,4096]{1,0:T(8,128)(2,1)S(1)}, bf16[32,4096]{1,0:T(8,128)(2,1)S(1)}, u32[]{:S(2)}, u32[]{:S(2)}) collective-permute-start(bf16[32,4096]{1,0:T(8,128)(2,1)S(1)} %copy-done.45), channel_id=1, source_target_pairs={{0,3},{1,2},{2,1},{3,0},{4,7},{5,6},{6,5},{7,4},{8,11},{9,10},{10,... | collective-permute-start | bytes 786440 | tf_op jit(solution)/shard_map/ppermute | solution.py:53
  (73 other events, 673.7 us)
